TPU v7x, 32 devices: a whole 2x2x4 slice. The times are simulated.
32 devices in a mesh: groups: 2 (over y), bricks: 4 (over z), chan: 2 (over x), rep: 2 (over core).
Axes of the slice: x: 2, y: 2, z: 4, core: 2. Of those that a mesh axis runs over, the one named last changes fastest.
Arguments:
- features: bfloat16 [16, 64, 8, 24, 128], P(('groups', 'bricks', 'rep')), parts along dimension 0, may hold values from -6 to 6
- w_first: bfloat16 [27, 64, 64], P(None, None, 'chan'), may hold values from -0.15625 to 0.15625
- w_second: bfloat16 [27, 64, 64], P(None, None, 'chan'), may hold values from -0.15625 to 0.15625
- w_down: bfloat16 [8, 64, 64], P(None, 'chan'), may hold values from -0.25 to 0.25
- w_head: float32 [64], replicated, may hold values from -0.75 to 0.75
- footprint: int32 [2, 16], P(None, 'groups'), parts along dimension 1, may hold values from 0 to 3, as said below
- labels: int32 [16, 4, 768], P(('groups', 'bricks', 'rep')), parts along dimension 0, may hold values 0 or 1
Outputs:
- grad_second: float32 [54, 64, 64], P('groups', None, 'chan'), parts along dimension 0
- grad_down: float32 [16, 64, 64], P('groups', 'chan'), parts along dimension 0
- grad_head: float32 [128], P('groups'), parts along dimension 0
- loss: float32 [2], P('groups'), parts along dimension 0
There are 2 independent parts, one for each index of `groups`. A program takes and returns all parts, laid end to end along the dimension named above; an argument that names none is the same for every part. Nothing has to cross between parts.
Inputs may be any that keep to these rules, and one draw needn't show every extreme that they name: `footprint`: row 0 gives each column's first live brick row, 0 or 1; row 1 its number of live bricks. Columns 2k and 2k + 1 hold 2 to 4 live bricks together, and some column holds 3.
All inputs are finite; a program needn't handle non-finite values. No bound on the sum of `labels` on one device may be relied on, other than what follows from the above.
Results may differ from a plain program's by a relative error of at most 0.0035.
Values may be sent and summed in bfloat16 or wider, within the bound.
No kernel may reach another device: no remote copies, remote signals or barrier semaphores. Data moves between devices by JAX's collectives and lax.ppermute only.
A program may use at most 128 MiB of HBM per device.

v0:
```python
import jax
import jax.numpy as jnp
from jax import lax
from jax.experimental import pallas as pl
from jax.experimental.pallas import tpu as pltpu
from jax.sharding import PartitionSpec as P

BRICK = 8
COARSE = 1024
ROWS = 256
F32 = jnp.float32
BF16 = jnp.bfloat16


def lanes_low(shape):
    return lax.broadcasted_iota(jnp.int32, shape, len(shape) - 1) % 128 < 64


def merge_half(low, high):
    return jnp.where(lanes_low(low.shape), low, high)


def shifted(value, by):
    row = lax.broadcasted_iota(jnp.int32, value.shape, 0) % 128
    inside = row >= by if by > 0 else row < 128 + by
    return jnp.where(inside, pltpu.roll(value, by % value.shape[0], 0), 0.0)


def build_conv(w_ref, out_ref):
    zero = jnp.zeros((64, 128), BF16)
    for e in range(3):
        for k in range(4):
            for slot, d in enumerate((0, 1, 2, -1)):
                for rx in range(2):
                    a = k - rx
                    halves = []
                    for ry in range(2):
                        b = d - ry + 1
                        live = 0 <= a < 3 and 0 <= b < 3
                        halves.append(w_ref[9 * a + 3 * b + e] if live else zero)
                    row = k * 256 + slot * 64
                    out_ref[e, row : row + 64, rx * 128 : rx * 128 + 128] = merge_half(*halves)


def plane_pairs(window_ref, first, pairs, slot=()):
    blocks = [window_ref[(*slot, pl.ds(first + 2 * k, 2))].reshape(2 * ROWS, 256) for k in range(pairs)]
    return jnp.concatenate(blocks, axis=1)


def conv_rows(lhs, mats):
    below, level, above = [jnp.dot(lhs, mat, preferred_element_type=F32) for mat in mats]
    return level + shifted(below, 2) + shifted(above, -2)


def half_mats(mat_ref, half):
    rows = pl.ds(pl.multiple_of(512 * half, 512), 512)
    return [mat_ref[e, rows, :] for e in range(3)]


def neighbour(foot_ref, column, columns, side):
    other = column + 2 * side - 1
    present = (other >= 0) & (other < columns)
    other = jnp.clip(other, 0, columns - 1)
    count = jnp.where(present, 2 * foot_ref[1, other], 0)
    return count, 2 * (foot_ref[0, other] - foot_ref[0, column])


def rims(count, offset, other_count, work):
    def rim(i, carry):
        t = jnp.where(i == 0, -1, count)

        @pl.when((t - offset >= 0) & (t - offset < other_count))
        def _():
            work(t)

        return carry

    lax.fori_loop(0, 2, rim, 0)


def gated(ref, plane, index, count):
    inside = (index >= 0) & (index < count)
    block = ref[plane, jnp.clip(index, 0, ref.shape[1] - 1)]
    return jnp.where(inside, block, jnp.zeros_like(block))


def turn_block(src_ref, dst_ref, plane, t):
    for py in range(2):
        tall = jnp.concatenate([src_ref[plane, 4 * t + py], src_ref[plane, 4 * t + 2 + py]], axis=0)
        dst_ref[plane, t, 128 * py : 128 * py + 128] = tall.T


def fill_window(window_ref, plane, src_ref, src_plane, index, count):
    window_ref[plane, :, 0:128] = gated(src_ref, src_plane, index, count)
    window_ref[plane, :, 128:256] = merge_half(
        gated(src_ref, src_plane, index + 1, count), gated(src_ref, src_plane, index - 1, count)
    )


def pack_kernel(w1_ref, w2_ref, wd_ref, out_ref):
    half = w1_ref.shape[1] // 2
    start = 0
    for ref in (w1_ref, w2_ref, wd_ref):
        stop = start + ref.shape[0]
        out_ref[start:stop] = jnp.concatenate([ref[:, :half], ref[:, half:]], axis=2)
        start = stop


def local_kernel(foot_ref, feat_ref, *refs):
    chans = lax.axis_size("chan")
    piece_refs = refs[:chans]
    part_ref, y1_ref, m1_ref, m2_ref, down_ref, back_ref, whole, turned, arranged = refs[chans:-2]
    even_window, odd_window = refs[-2:]
    column = lax.axis_index("bricks") * lax.axis_size("rep") + lax.axis_index("rep")
    me = lax.axis_index("chan")
    side = me * (BRICK // chans) // 4
    count = 2 * foot_ref[1, column]
    columns = lax.axis_size("bricks") * lax.axis_size("rep")
    other_count, offset = neighbour(foot_ref, column, columns, side)

    half = piece_refs[0].shape[1]
    for step in range(chans):
        block = piece_refs[step][...]
        source = lax.rem(me - step + chans, chans)
        for h in range(2):
            part = block[:, :, 64 * h : 64 * h + 64]
            rows = pl.ds(pl.multiple_of((2 * source + h) * half, half), half)
            whole[:, rows, :] = jnp.concatenate([part, part], axis=2)
    for t in range(54):
        turned[t] = jnp.concatenate([whole[t], whole[t]], axis=0).T[0:64]
    build_conv(turned.at[0:27], m1_ref)
    build_conv(turned.at[27:54], m2_ref)
    low = lanes_low((64, 128))
    zero = jnp.zeros((64, 128), BF16)
    for t in range(8):
        ab, e = t // 2, t % 2
        block = whole[54 + t]
        tile = jnp.concatenate([jnp.where(low, block, zero), jnp.where(low, zero, block)], axis=0)
        down_ref[ab * 128 : ab * 128 + 128, e * 128 : e * 128 + 128] = tile
        back_ref[:, t * 128 : t * 128 + 128] = tile.T

    def turn(t, carry):
        for p in range(8):
            turn_block(feat_ref, arranged, p, t)
        return carry

    lax.fori_loop(0, count, turn, 0)

    def fill(window, t):
        for p in range(8):
            fill_window(window, p, arranged, p, t, count)

    def edge(window, t):
        lhs = plane_pairs(window, 4 * side, 2)
        part_ref[t + 1] = conv_rows(lhs, half_mats(m1_ref, 1 - side))

    def conv(window, t):
        edge(window, t)
        lhs = plane_pairs(window, 0, 4)
        out = jnp.maximum(conv_rows(lhs, [m1_ref[e] for e in range(3)]), 0.0).astype(BF16)
        for par in range(2):
            for rx in range(2):
                y1_ref[2 * rx + par, t] = out[ROWS * par : ROWS * par + ROWS, 128 * rx : 128 * rx + 128]

    def pair(j, carry):
        fill(odd_window, 2 * j + 1)
        conv(even_window, 2 * j)
        fill(even_window, 2 * j + 2)
        conv(odd_window, 2 * j + 1)
        return carry

    def beside(t):
        fill(even_window, t)
        edge(even_window, t)

    rims(count, offset, other_count, beside)
    fill(even_window, 0)
    lax.fori_loop(0, count // 2, pair, 0)


def main_kernel(
    foot_ref,
    part_ref,
    halo_ref,
    near_ref,
    m1_ref,
    m2_ref,
    down_mat,
    back_mat,
    head_ref,
    label_ref,
    keep_ref,
    send_ref,
    arranged,
    even_window,
    odd_window,
    hidden,
    hwin,
    headm_ref,
    y2_ref,
    delta_t,
    err_t,
    grad,
    grad_down,
    small,
    whole,
):
    reps, chans = lax.axis_size("rep"), lax.axis_size("chan")
    columns = lax.axis_size("bricks") * reps
    column = lax.axis_index("bricks") * reps + lax.axis_index("rep")
    planes = BRICK // chans
    mine = lax.axis_index("chan") * planes
    side = mine // 4
    count = 2 * foot_ref[1, column]
    other_count, offset = neighbour(foot_ref, column, columns, side)

    grad[...] = jnp.zeros_like(grad)
    grad_down[...] = jnp.zeros_like(grad_down)
    small[...] = jnp.zeros_like(small)
    head_row = jnp.concatenate([head_ref[...], head_ref[...]], axis=1)
    square_row = lax.broadcasted_iota(jnp.int32, (128, 128), 0)
    square_lane = lax.broadcasted_iota(jnp.int32, (128, 128), 1)
    same_half = (square_row < 64) == (square_lane < 64)
    head_mat = jnp.where(same_half, jnp.broadcast_to(head_row, (128, 128)).T, 0.0)
    head_high = head_mat.astype(BF16)
    headm_ref[0:128] = head_high
    headm_ref[128:256] = head_high
    headm_ref[256:384] = (head_mat - head_high.astype(F32)).astype(BF16)
    pick_depth = jnp.where(square_row // 2 == square_lane % 64, 1.0, 0.0).astype(BF16)

    def turn(t, carry):
        for p in range(4):
            turn_block(halo_ref, arranged, p, t)
        return carry

    lax.fori_loop(0, other_count, turn, 0)

    def fill(window, t):
        for p in range(4):
            fill_window(window, p, arranged, p, t - offset, other_count)

    def first(window, t):
        own = (t >= 0) & (t < count)
        next_to = (t - offset >= 0) & (t - offset < other_count)
        out = part_ref[t + 1] + conv_rows(plane_pairs(window, 0, 2), half_mats(m1_ref, side))
        out = jnp.maximum(out, 0.0).astype(BF16)
        for rx in range(2):
            live = jnp.where(side == rx, next_to, own)
            for par in range(2):
                block = out[ROWS * par : ROWS * par + ROWS, 128 * rx : 128 * rx + 128]
                hidden[t + 1, side * 4 + 2 * rx + par] = jnp.where(live, block, jnp.zeros_like(block))

    def near(t):
        for p in range(4):
            hidden[t + 1, (1 - side) * 4 + p] = gated(near_ref, p, t, count)

    def beside(t):
        fill(even_window, t)
        first(even_window, t)

    def pair(j, carry):
        fill(odd_window, 2 * j + 1)
        near(2 * j)
        first(even_window, 2 * j)
        fill(even_window, 2 * j + 2)
        near(2 * j + 1)
        first(odd_window, 2 * j + 1)
        return carry

    hidden[0] = jnp.zeros((8, ROWS, 128), BF16)
    hidden[count + 1] = jnp.zeros((8, ROWS, 128), BF16)
    rims(count, offset, other_count, beside)
    fill(even_window, 0)
    lax.fori_loop(0, count // 2, pair, 0)

    row4 = lax.broadcasted_iota(jnp.int32, (512, 128), 0)
    even4 = row4 % 2 == 0
    plane4 = 4 * side + 2 * (row4 // 128 % 2)
    keep = even4 & (plane4 >= mine) & (plane4 < mine + planes)

    def second(j, carry):
        for u in range(2):
            t = 2 * j + u
            for p in range(8):
                hwin[u, p, :, 0:128] = hidden[t + 1, p]
                hwin[u, p, :, 128:256] = merge_half(hidden[t + 2, p], hidden[t, p])
            out = conv_rows(plane_pairs(hwin, 0, 4, (u,)), [m2_ref[e] for e in range(3)])
            out = jnp.maximum(out, 0.0).astype(BF16)
            for par in range(2):
                for rx in range(2):
                    y2_ref[u, rx, par] = out[ROWS * par : ROWS * par + ROWS, 128 * rx : 128 * rx + 128]
        fine = jnp.concatenate(
            [
                jnp.concatenate(
                    [y2_ref[u, rx, a, 128 * b : 128 * b + 128] for u in range(2) for rx in range(2)],
                    axis=0,
                )
                for a in range(2)
                for b in range(2)
            ],
            axis=1,
        )
        both = jnp.dot(fine, down_mat[...], preferred_element_type=F32)
        coarse = both[:, 0:128] + shifted(both[:, 128:256], -1)
        rect = jnp.maximum(coarse, 0.0)
        high = rect.astype(BF16)
        rest = (rect - high.astype(F32)).astype(BF16)
        logit = jnp.dot(
            jnp.concatenate([high, rest, high], axis=1), headm_ref[...], preferred_element_type=F32
        )
        labels = []
        for u in range(2):
            line = label_ref[:, pl.ds(pl.multiple_of(256 * j + 128 * u, 128), 128)].astype(F32)
            for rx in range(2):
                row = jnp.where(side == 1, line[2 + rx : 3 + rx], line[rx : rx + 1])
                row = jnp.where(same_half, jnp.broadcast_to(row, (128, 128)), 0.0).astype(BF16)
                labels.append(
                    lax.dot_general(
                        pick_depth, row, (((1,), (1,)), ((), ())), preferred_element_type=F32
                    )
                )
        label = jnp.concatenate(labels, axis=0)
        tail = jnp.exp(-jnp.abs(logit))
        soft = jnp.maximum(logit, 0.0) + jnp.log1p(tail)
        sigmoid = jnp.where(logit >= 0.0, 1.0, tail) / (1.0 + tail)
        loss = jnp.where(keep, soft - label * logit, 0.0)
        slope = jnp.where(keep, (sigmoid - label) * (1.0 / COARSE), 0.0)
        small[0:1] += jnp.sum(slope * rect, axis=0, keepdims=True)
        small[1:2] += jnp.sum(loss, axis=0, keepdims=True)
        delta = jnp.where(coarse > 0.0, slope * head_row, 0.0).astype(BF16).astype(F32)
        moved = shifted(delta, 1)
        delta_t[0:128] = delta.astype(BF16).T
        delta_t[128:256] = moved.astype(BF16).T
        back = jnp.dot((delta + moved).astype(BF16), back_mat[...], preferred_element_type=F32)
        for a in range(2):
            for b in range(2):
                lane = (2 * a + b) * 256
                err = jnp.where(even4, back[:, lane : lane + 128], back[:, lane + 128 : lane + 256])
                live = fine[:, lane // 2 : lane // 2 + 128].astype(F32) > 0.0
                err = jnp.where(live, err, 0.0)
                for n in range(4):
                    turned = err[128 * n : 128 * n + 128].astype(BF16).T
                    col = n * 512 + a * 256 + b * 128
                    err_t[128:256, col : col + 128] = turned
                    up = jnp.where(square_lane < 126, pltpu.roll(turned, 126, 1), jnp.zeros_like(turned))
                    down = jnp.where(square_lane >= 2, pltpu.roll(turned, 2, 1), jnp.zeros_like(turned))
                    err_t[0:128, col : col + 128] = up
                    err_t[256:384, col : col + 128] = down
        grad_down[...] += jnp.dot(delta_t[...], fine, preferred_element_type=F32)
        for a in range(3):
            rows = hwin[:, 2 * a : 2 * a + 4].reshape(8 * ROWS, 256)
            grad[a] += jnp.dot(err_t[...], rows, preferred_element_type=F32)
        return carry

    lax.fori_loop(0, count // 2, second, 0)

    low = lanes_low((64, 128))
    rep, chan = lax.axis_index("rep"), lax.axis_index("chan")
    share = 64 // chans // reps

    def emit(slab, value):
        whole[slab] = value

    firsts = []
    for a in range(3):
        for e in range(3):
            both = grad[a, 128 * e : 128 * e + 64] + pltpu.roll(
                grad[a, 128 * e + 64 : 128 * e + 128], 192, 1
            )
            emit(3 * a + e, both[:, 0:128])
            firsts.append(both[:, 128:256])
    for m in range(5):
        right = firsts[2 * m + 1] if 2 * m + 1 < 9 else jnp.zeros_like(firsts[0])
        emit(9 + m, jnp.where(low, pltpu.roll(firsts[2 * m], 64, 1), right))
    halves = [
        grad_down[128 * e : 128 * e + 64] + pltpu.roll(grad_down[128 * e + 64 : 128 * e + 128], 448, 1)
        for e in range(2)
    ]
    for ab in range(4):
        tile = jnp.concatenate([half[:, 128 * ab : 128 * ab + 128] for half in halves], axis=0)
        emit(14 + ab, tile.T[0:64])
    sums = small[...]
    head = sums[0:1] + pltpu.roll(sums, 64, 1)[0:1]
    total = jnp.sum(sums[1:2], axis=1, keepdims=True) * (1.0 / 64)
    row = merge_half(head, jnp.broadcast_to(total, (1, 128)))
    emit(18, jnp.broadcast_to(row, (64, 128)))
    for c in range(chans):
        place = lax.rem(c - chan + chans, chans)
        for ref, r in ((keep_ref, rep), (send_ref, 1 - rep)):
            rows = pl.ds(pl.multiple_of((c * reps + r) * share, share), share)
            ref[place] = whole[:, rows, :]


def final_kernel(foot_ref, mine_ref, peer_ref, second_ref, down_ref, head_ref, loss_ref):
    rep = lax.axis_index("rep")
    share = mine_ref.shape[1]
    for ref, r in ((mine_ref, rep), (peer_ref, 1 - rep)):
        rows = pl.ds(pl.multiple_of(r * share, share), share)
        for a in range(3):
            for e in range(3):
                m = 3 * a + e
                later, first = ref[m], ref[9 + m // 2]
                second_ref[9 * a + e, rows] = first[:, 64 * (m % 2) : 64 * (m % 2) + 64]
                second_ref[9 * a + 3 + e, rows] = later[:, 0:64]
                second_ref[9 * a + 6 + e, rows] = later[:, 64:128]
        for ab in range(4):
            for e in range(2):
                down_ref[2 * ab + e, rows] = ref[14 + ab][:, 64 * e : 64 * e + 64]
    line = mine_ref[18][0:1]
    head_ref[...] = line[:, 0:64]
    live = foot_ref[1, 0]
    for c in range(1, foot_ref.shape[1]):
        live += foot_ref[1, c]
    scale = jnp.full((1, 1), COARSE * live, jnp.int32).astype(F32)
    loss_ref[...] = line[:, 64:65] / scale


def sums_slab(shape):
    return lax.broadcasted_iota(jnp.int32, shape, 0) == 18


def to_wire(value):
    high = lax.reduce_precision(value, 8, 7)
    rest = lax.reduce_precision(value - high, 8, 7)
    lower = lax.broadcasted_iota(jnp.int32, value.shape, 1) >= value.shape[1] // 2
    return jnp.where(sums_slab(value.shape) & lower, rest, high)


def from_wire(value):
    half = value.shape[1] // 2
    other = jnp.concatenate([value[:, half:], value[:, :half]], axis=1)
    return value + jnp.where(sums_slab(value.shape), other, 0.0)


def shards(features, w_first, w_second, w_down, w_head, footprint, labels):
    bricks, chans, reps = lax.axis_size("bricks"), lax.axis_size("chan"), lax.axis_size("rep")
    planes = BRICK // chans
    side = lax.axis_index("chan") * planes // 4
    smem = pl.BlockSpec(memory_space=pltpu.SMEM)
    vmem = pl.BlockSpec(memory_space=pltpu.VMEM)
    features = features[0]
    slabs = features.shape[2] // 4

    packed = pl.pallas_call(
        pack_kernel,
        out_shape=jax.ShapeDtypeStruct((62, 32 // chans, 128), BF16),
        in_specs=[vmem] * 3,
        out_specs=vmem,
        compiler_params=pltpu.CompilerParams(vmem_limit_bytes=16 << 20),
        name="pack",
    )(w_first.transpose(0, 2, 1), w_second.transpose(0, 2, 1), w_down)
    pieces = [packed]
    for step in range(1, chans):
        ring = [(i, (i + step) % chans) for i in range(chans)]
        pieces.append(lax.ppermute(packed, "chan", ring))

    pairs = []
    for col in range(bricks * reps):
        for c in range(chans):
            src = col + 2 * (c * planes // 4) - 1
            if 0 <= src < bricks * reps:
                ends = [(j // reps * chans + c) * reps + j % reps for j in (src, col)]
                pairs.append(tuple(ends))
    outward = lax.dynamic_slice_in_dim(features, (1 - side) * 4, 4, 1).transpose(1, 2, 0, 3)
    halo = lax.ppermute(outward, ("bricks", "chan", "rep"), pairs)

    part, near, mat1, mat2, down_mat, back_mat = pl.pallas_call(
        local_kernel,
        out_shape=(
            jax.ShapeDtypeStruct((slabs + 2, 2 * ROWS, 256), F32),
            jax.ShapeDtypeStruct((4, slabs, ROWS, 128), BF16),
            jax.ShapeDtypeStruct((3, 1024, 256), BF16),
            jax.ShapeDtypeStruct((3, 1024, 256), BF16),
            jax.ShapeDtypeStruct((512, 256), BF16),
            jax.ShapeDtypeStruct((128, 1024), BF16),
        ),
        in_specs=[smem] + [vmem] * (1 + chans),
        out_specs=(vmem,) * 6,
        scratch_shapes=[
            pltpu.VMEM((62, 64, 128), BF16),
            pltpu.VMEM((54, 64, 128), BF16),
            pltpu.VMEM((8, slabs, ROWS, 128), BF16),
            pltpu.VMEM((8, ROWS, 256), BF16),
            pltpu.VMEM((8, ROWS, 256), BF16),
        ],
        compiler_params=pltpu.CompilerParams(vmem_limit_bytes=36 << 20),
        cost_estimate=pl.CostEstimate(flops=6 * 6 * 512 * 1024 * 512, bytes_accessed=8 << 20, transcendentals=0),
        name="first_local",
    )(footprint, features.transpose(1, 2, 0, 3), *pieces)
    parts = jax.ShapeDtypeStruct((chans, 19, 64 // chans // reps, 128), F32)
    keep, send = pl.pallas_call(
        main_kernel,
        out_shape=(parts, parts),
        in_specs=[smem] + [vmem] * 9,
        out_specs=(vmem, vmem),
        scratch_shapes=[
            pltpu.VMEM((4, slabs, ROWS, 128), BF16),
            pltpu.VMEM((4, ROWS, 256), BF16),
            pltpu.VMEM((4, ROWS, 256), BF16),
            pltpu.VMEM((slabs + 2, 8, ROWS, 128), BF16),
            pltpu.VMEM((2, 8, ROWS, 256), BF16),
            pltpu.VMEM((384, 128), BF16),
            pltpu.VMEM((2, 2, 2, ROWS, 128), BF16),
            pltpu.VMEM((256, 512), BF16),
            pltpu.VMEM((384, 2048), BF16),
            pltpu.VMEM((3, 384, 256), F32),
            pltpu.VMEM((256, 512), F32),
            pltpu.VMEM((8, 128), F32),
            pltpu.VMEM((19, 64, 128), F32),
        ],
        compiler_params=pltpu.CompilerParams(vmem_limit_bytes=40 << 20),
        cost_estimate=pl.CostEstimate(flops=4 * 6 * 6 * 512 * 1024 * 512, bytes_accessed=16 << 20, transcendentals=0),
        name="head_and_grads",
    )(footprint, part, halo, near, mat1, mat2, down_mat, back_mat, w_head.reshape(1, 64), labels[0])

    swap = [(i, 1 - i) for i in range(reps)]
    got = lax.ppermute(send, "rep", swap)
    wire = [to_wire(keep[step] + got[step]) for step in range(chans)]
    near_sums = []
    for flip in range(2):
        for step in range(chans):
            if flip == step == 0:
                near_sums.append(wire[0])
                continue
            routes = [
                (b * chans + c, (b ^ flip) * chans + (c + step) % chans)
                for b in range(bricks)
                for c in range(chans)
            ]
            sent = lax.ppermute(wire[step].astype(BF16), ("bricks", "chan"), routes)
            near_sums.append(sent.astype(F32))
    mine = from_wire(sum(near_sums[1:chans], near_sums[0]) + sum(near_sums[chans + 1 :], near_sums[chans]))
    step = 2
    while step < bricks:
        wire = to_wire(mine)
        sent = lax.ppermute(wire.astype(BF16), "bricks", [(i, i ^ step) for i in range(bricks)])
        mine = from_wire(wire + sent.astype(F32))
        step *= 2
    peer = lax.ppermute(mine, "rep", swap)
    share = 64 // chans
    second, down, head, loss = pl.pallas_call(
        final_kernel,
        out_shape=(
            jax.ShapeDtypeStruct((27, share, 64), F32),
            jax.ShapeDtypeStruct((8, share, 64), F32),
            jax.ShapeDtypeStruct((1, 64), F32),
            jax.ShapeDtypeStruct((1, 1), F32),
        ),
        in_specs=[smem, vmem, vmem],
        out_specs=(vmem,) * 4,
        compiler_params=pltpu.CompilerParams(vmem_limit_bytes=16 << 20),
        name="assemble",
    )(footprint, mine, peer)
    return second.transpose(0, 2, 1), down, head.reshape(64), loss.reshape(1)


def solution(mesh):
    return jax.shard_map(
        shards,
        mesh=mesh,
        in_specs=(
            P(("groups", "bricks", "rep"), None, None, None, None),
            P(None, None, "chan"),
            P(None, None, "chan"),
            P(None, "chan", None),
            P(),
            P(None, "groups"),
            P(("groups", "bricks", "rep"), None, None),
        ),
        out_specs=(P("groups", None, "chan"), P("groups", "chan", None), P("groups"), P("groups")),
        check_vma=False,
    )
```

profile of v0, /device:TPU:0, one launch (start us, length us, event | category | flops | bytes accessed | tf_op | source)
XLA Modules:
  0.0 67.6 jit_solution(9477760792779771018)
XLA Ops:
  0.6 1.7 %constant_dynamic-slice_fusion = bf16[1,64,4,24,128]{4,3,2,1,0:T(8,128)(2,1)S(1)} fusion(bf16[1,64,8,24,128]{4,3,2,1,0:T(8,128)(2,1)} %param.7, s32[]{:T(128)S(6)} %select_n.26), kind=kLoop, calls=%fused_computation.24 | loop fusion | bytes 3145732 | tf_op jit(solution)/shard_map/dynamic_slice | solution.py:464
  2.3 0.0 copy-start
  2.4 0.0 copy-start.1
  2.4 0.0 copy-start.2
  2.4 0.0 copy-start.6
  2.4 0.6 copy.16
  3.0 2.6 %collective-permute-start.1 = (bf16[4,24,64,128]{3,2,1,0:T(8,128)(2,1)S(1)}, bf16[4,24,64,128]{3,2,1,0:T(8,128)(2,1)S(1)}, u32[]{:S(2)}, u32[]{:S(2)}) collective-permute-start(bf16[4,24,64,128]{3,2,1,0:T(8,128)(2,1)S(1)} %bitcast.34), channel_id=1, source_target_pairs={{3,2},{0,1},{6,3},{1,4},{7,6},{4,5},{10,7},{5,8},{11,10},{8,9},{14... | collective-permute-start | bytes 4718600 | tf_op jit(solution)/shard_map/ppermute | solution.py:465
  5.6 0.0 copy-done
  5.6 0.0 copy-done.1
  5.6 0.0 copy-done.2
  5.6 0.1 pack.1.refs_0_
  5.8 0.0 copy-start.3
  5.8 1.8 %collective-permute-start = (bf16[62,16,128]{2,1,0:T(8,128)(2,1)S(1)}, bf16[62,16,128]{2,1,0:T(8,128)(2,1)S(1)}, u32[]{:S(2)}, u32[]{:S(2)}) collective-permute-start(bf16[62,16,128]{2,1,0:T(8,128)(2,1)S(1)} %pack.1.refs_0_), channel_id=1, source_target_pairs={{0,2},{2,0},{1,3},{3,1},{4,6},{6,4},{5,7},{7,5},{8,10},{10,8},{9,1... | collective-permute-start | bytes 761864 | tf_op jit(solution)/shard_map/ppermute | solution.py:455
  7.6 0.0 copy-done.6
  7.6 2.0 %copy.15 = bf16[1,64,8,24,128]{4,1,3,2,0:T(8,128)(2,1)S(1)} copy(bf16[1,64,8,24,128]{4,3,2,1,0:T(8,128)(2,1)S(1)} %copy-done.6) | data formatting | bytes 6291456 | tf_op args[0]
  9.7 4.3 %collective-permute-done.refs_1_ = bf16[62,16,128]{2,1,0:T(8,128)(2,1)S(1)} collective-permute-done((bf16[62,16,128]{2,1,0:T(8,128)(2,1)S(1)}, bf16[62,16,128]{2,1,0:T(8,128)(2,1)S(1)}, u32[]{:S(2)}, u32[]{:S(2)}) %collective-permute-start) | collective-permute-done | bytes 253984 | tf_op jit(solution)/shard_map/ppermute | solution.py:455
  14.0 0.0 copy-done.3
  14.0 0.0 copy-start.4
  14.0 0.0 copy-start.5
  14.0 5.2 %first_local.1 = (f32[8,512,256]{2,1,0:T(8,128)S(1)}, bf16[4,6,256,128]{3,2,1,0:T(8,128)(2,1)S(1)}, bf16[3,1024,256]{2,1,0:T(8,128)(2,1)S(1)}, bf16[3,1024,256]{...) custom-call(s32[2,8]{1,0:T(2,128)S(1)} %copy-done.3, ...), custom_call_target="tpu_custom_call" | custom-call | flops 9663676416 | bytes 8388608 | tf_op jit(solution)/shard_map/first_local/pallas_call | solution.py:467
  19.2 0.0 collective-permute-done.1.halo_ref
  19.2 0.0 copy-done.4
  19.2 0.0 copy-done.5
  19.2 8.2 %head_and_grads.1 = (f32[2,19,16,128]{3,2,1,0:T(8,128)S(1)}, f32[2,19,16,128]{3,2,1,0:T(8,128)S(1)}) custom-call(s32[2,8]{1,0:T(2,128)S(1)} %copy-done.3, f32[8,512,256]{2,1,0:T(8,128)S(1)} %get-tuple-element.16.part_ref, bf16[4,24,64,128]{3,2,1,0:T(8,128)(2,1)S(1)} %collective-permute-done.1.halo_ref, ...), custom_call_target="tpu_custom_call" | custom-call | flops 38654705664 | bytes 16777216 | tf_op jit(solution)/shard_map/head_and_grads/pallas_call | solution.py:491
  27.5 12.9 %collective-permute-start.2 = (f32[2,19,16,128]{3,2,1,0:T(8,128)S(1)}, f32[2,19,16,128]{3,2,1,0:T(8,128)S(1)}, u32[]{:S(2)}, u32[]{:S(2)}) collective-permute-start(f32[2,19,16,128]{3,2,1,0:T(8,128)S(1)} %get-tuple-element.23), channel_id=1, source_target_pairs={{0,1},{1,0},{2,3},{3,2},{4,5},{5,4},{6,7},{7,6},{8,9},{9,8},{10,11... | collective-permute-start | bytes 933896 | tf_op jit(solution)/shard_map/ppermute | solution.py:517
  40.4 1.2 %collective-permute-done.2 = f32[2,19,16,128]{3,2,1,0:T(8,128)S(1)} collective-permute-done((f32[2,19,16,128]{3,2,1,0:T(8,128)S(1)}, f32[2,19,16,128]{3,2,1,0:T(8,128)S(1)}, u32[]{:S(2)}, u32[]{:S(2)}) %collective-permute-start.2) | collective-permute-done | bytes 311328 | tf_op jit(solution)/shard_map/ppermute | solution.py:517
  41.6 0.1 fusion.8
  41.7 10.8 %collective-permute-start.5 = (bf16[19,16,128]{2,1,0:T(8,128)(2,1)S(1)}, bf16[19,16,128]{2,1,0:T(8,128)(2,1)S(1)}, u32[]{:S(2)}, u32[]{:S(2)}) collective-permute-start(bf16[19,16,128]{2,1,0:T(8,128)(2,1)S(1)} %get-tuple-element.29), channel_id=1, source_target_pairs={{0,6},{2,4},{4,2},{6,0},{8,14},{10,12},{12,10},{14,8},{1,7},{3,5},... | collective-permute-start | bytes 233480 | tf_op jit(solution)/shard_map/ppermute | solution.py:530
  52.6 0.0 collective-permute-start.4
  52.6 0.6 collective-permute-start.3
  53.2 2.2 %collective-permute-done.5 = bf16[19,16,128]{2,1,0:T(8,128)(2,1)S(1)} collective-permute-done((bf16[19,16,128]{2,1,0:T(8,128)(2,1)S(1)}, bf16[19,16,128]{2,1,0:T(8,128)(2,1)S(1)}, u32[]{:S(2)}, u32[]{:S(2)}) %collective-permute-start.5) | collective-permute-done | bytes 77856 | tf_op jit(solution)/shard_map/ppermute | solution.py:530
  55.4 1.5 %collective-permute-done.4 = bf16[19,16,128]{2,1,0:T(8,128)(2,1)S(1)} collective-permute-done((bf16[19,16,128]{2,1,0:T(8,128)(2,1)S(1)}, bf16[19,16,128]{2,1,0:T(8,128)(2,1)S(1)}, u32[]{:S(2)}, u32[]{:S(2)}) %collective-permute-start.4) | collective-permute-done | bytes 77856 | tf_op jit(solution)/shard_map/ppermute | solution.py:530
  57.0 0.0 collective-permute-done.3
  57.0 0.1 add_add_fusion
  57.1 0.1 fusion.9
  57.2 3.2 %collective-permute-start.6 = (bf16[19,16,128]{2,1,0:T(8,128)(2,1)S(1)}, bf16[19,16,128]{2,1,0:T(8,128)(2,1)S(1)}, u32[]{:S(2)}, u32[]{:S(2)}) collective-permute-start(bf16[19,16,128]{2,1,0:T(8,128)(2,1)S(1)} %fusion.9), channel_id=1, source_target_pairs={{0,8},{4,12},{8,0},{12,4},{1,9},{5,13},{9,1},{13,5},{2,10},{6,14},... | collective-permute-start | bytes 233480 | tf_op jit(solution)/shard_map/ppermute | solution.py:536
  60.4 4.0 %collective-permute-done.6 = bf16[19,16,128]{2,1,0:T(8,128)(2,1)S(1)} collective-permute-done((bf16[19,16,128]{2,1,0:T(8,128)(2,1)S(1)}, bf16[19,16,128]{2,1,0:T(8,128)(2,1)S(1)}, u32[]{:S(2)}, u32[]{:S(2)}) %collective-permute-start.6) | collective-permute-done | bytes 77856 | tf_op jit(solution)/shard_map/ppermute | solution.py:536
  64.4 0.1 convert_add_fusion
  64.5 0.1 fusion.7.mine_ref
  64.6 0.1 collective-permute-start.7
  64.7 1.4 %collective-permute-done.7.peer_ref = f32[19,16,128]{2,1,0:T(8,128)S(1)} collective-permute-done((f32[19,16,128]{2,1,0:T(8,128)S(1)}, f32[19,16,128]{2,1,0:T(8,128)S(1)}, u32[]{:S(2)}, u32[]{:S(2)}) %collective-permute-start.7) | collective-permute-done | bytes 155680 | tf_op jit(solution)/shard_map/ppermute | solution.py:539
  66.1 1.5 %assemble.1 = (f32[27,32,64]{2,1,0:T(8,128)}, f32[8,32,64]{2,1,0:T(8,128)}, f32[1,64]{1,0:T(1,128)}, f32[1,1]{1,0:T(1,128)}) custom-call(s32[2,8]{1,0:T(2,128)S(1)} %copy-done.3, f32[19,16,128]{2,1,0:T(8,128)S(1)} %fusion.7.mine_ref, f32[19,16,128]{2,1,0:T(8,128)S(1)} %collective-permute-done.7.peer_ref), custom_call_target="tpu_custom_call" | custom-call | tf_op jit(solution)/shard_map/assemble/pallas_call | solution.py:541
  (4 shorter events, 0.0 us)
Async XLA Ops:
  2.3 3.3 %copy-start = (bf16[27,64,32]{1,2,0:T(8,128)(2,1)S(1)}, bf16[27,64,32]{1,2,0:T(8,128)(2,1)}, u32[]{:S(2)}) copy-start(bf16[27,64,32]{1,2,0:T(8,128)(2,1)} %param.8) | copy-start | bytes 331780
  2.4 3.3 %copy-start.1 = (bf16[27,64,32]{1,2,0:T(8,128)(2,1)S(1)}, bf16[27,64,32]{1,2,0:T(8,128)(2,1)}, u32[]{:S(2)}) copy-start(bf16[27,64,32]{1,2,0:T(8,128)(2,1)} %param.9) | copy-start | bytes 331780
  2.4 3.3 %copy-start.2 = (bf16[8,32,64]{2,1,0:T(8,128)(2,1)S(1)}, bf16[8,32,64]{2,1,0:T(8,128)(2,1)}, u32[]{:S(2)}) copy-start(bf16[8,32,64]{2,1,0:T(8,128)(2,1)} %wd_ref.1) | copy-start | bytes 98308
  2.4 5.2 %copy-start.6 = (bf16[1,64,8,24,128]{4,3,2,1,0:T(8,128)(2,1)S(1)}, bf16[1,64,8,24,128]{4,3,2,1,0:T(8,128)(2,1)}, u32[]{:S(2)}) copy-start(bf16[1,64,8,24,128]{4,3,2,1,0:T(8,128)(2,1)} %param.7) | copy-start | bytes 9437188
  3.0 16.2 %collective-permute-start.1 = (bf16[4,24,64,128]{3,2,1,0:T(8,128)(2,1)S(1)}, bf16[4,24,64,128]{3,2,1,0:T(8,128)(2,1)S(1)}, u32[]{:S(2)}, u32[]{:S(2)}) collective-permute-start(bf16[4,24,64,128]{3,2,1,0:T(8,128)(2,1)S(1)} %bitcast.34), channel_id=1, source_target_pairs={{3,2},{0,1},{6,3},{1,4},{7,6},{4,5},{10,7},{5,8},{11,10},{8,9},{14... | collective-permute-start | bytes 4718600 | tf_op jit(solution)/shard_map/ppermute | solution.py:465
  5.8 8.2 %copy-start.3 = (s32[2,8]{1,0:T(2,128)S(1)}, s32[2,8]{1,0:T(2,128)}, u32[]{:S(2)}) copy-start(s32[2,8]{1,0:T(2,128)} %foot_ref.5) | copy-start | bytes 196
  5.8 8.2 %collective-permute-start = (bf16[62,16,128]{2,1,0:T(8,128)(2,1)S(1)}, bf16[62,16,128]{2,1,0:T(8,128)(2,1)S(1)}, u32[]{:S(2)}, u32[]{:S(2)}) collective-permute-start(bf16[62,16,128]{2,1,0:T(8,128)(2,1)S(1)} %pack.1.refs_0_), channel_id=1, source_target_pairs={{0,2},{2,0},{1,3},{3,1},{4,6},{6,4},{5,7},{7,5},{8,10},{10,8},{9,1... | collective-permute-start | bytes 761864 | tf_op jit(solution)/shard_map/ppermute | solution.py:455
  14.0 5.2 %copy-start.4 = (s32[1,4,768]{2,1,0:T(4,128)S(1)}, s32[1,4,768]{2,1,0:T(4,128)}, u32[]{:S(2)}) copy-start(s32[1,4,768]{2,1,0:T(4,128)} %param.13) | copy-start | bytes 36868
  14.0 5.2 %copy-start.5 = (f32[64]{0:T(128)S(1)}, f32[64]{0:T(128)}, u32[]{:S(2)}) copy-start(f32[64]{0:T(128)} %param.11) | copy-start | bytes 772
  27.5 14.2 %collective-permute-start.2 = (f32[2,19,16,128]{3,2,1,0:T(8,128)S(1)}, f32[2,19,16,128]{3,2,1,0:T(8,128)S(1)}, u32[]{:S(2)}, u32[]{:S(2)}) collective-permute-start(f32[2,19,16,128]{3,2,1,0:T(8,128)S(1)} %get-tuple-element.23), channel_id=1, source_target_pairs={{0,1},{1,0},{2,3},{3,2},{4,5},{5,4},{6,7},{7,6},{8,9},{9,8},{10,11... | collective-permute-start | bytes 933896 | tf_op jit(solution)/shard_map/ppermute | solution.py:517
  41.7 13.7 %collective-permute-start.5 = (bf16[19,16,128]{2,1,0:T(8,128)(2,1)S(1)}, bf16[19,16,128]{2,1,0:T(8,128)(2,1)S(1)}, u32[]{:S(2)}, u32[]{:S(2)}) collective-permute-start(bf16[19,16,128]{2,1,0:T(8,128)(2,1)S(1)} %get-tuple-element.29), channel_id=1, source_target_pairs={{0,6},{2,4},{4,2},{6,0},{8,14},{10,12},{12,10},{14,8},{1,7},{3,5},... | collective-permute-start | bytes 233480 | tf_op jit(solution)/shard_map/ppermute | solution.py:530
  52.6 4.4 %collective-permute-start.4 = (bf16[19,16,128]{2,1,0:T(8,128)(2,1)S(1)}, bf16[19,16,128]{2,1,0:T(8,128)(2,1)S(1)}, u32[]{:S(2)}, u32[]{:S(2)}) collective-permute-start(bf16[19,16,128]{2,1,0:T(8,128)(2,1)S(1)} %get-tuple-element.28), channel_id=1, source_target_pairs={{0,4},{2,6},{4,0},{6,2},{8,12},{10,14},{12,8},{14,10},{1,5},{3,7},... | collective-permute-start | bytes 233480 | tf_op jit(solution)/shard_map/ppermute | solution.py:530
  52.6 4.4 %collective-permute-start.3 = (bf16[19,16,128]{2,1,0:T(8,128)(2,1)S(1)}, bf16[19,16,128]{2,1,0:T(8,128)(2,1)S(1)}, u32[]{:S(2)}, u32[]{:S(2)}) collective-permute-start(bf16[19,16,128]{2,1,0:T(8,128)(2,1)S(1)} %get-tuple-element.29), channel_id=1, source_target_pairs={{0,2},{2,0},{4,6},{6,4},{8,10},{10,8},{12,14},{14,12},{1,3},{3,1},... | collective-permute-start | bytes 233480 | tf_op jit(solution)/shard_map/ppermute | solution.py:530
  57.2 7.1 %collective-permute-start.6 = (bf16[19,16,128]{2,1,0:T(8,128)(2,1)S(1)}, bf16[19,16,128]{2,1,0:T(8,128)(2,1)S(1)}, u32[]{:S(2)}, u32[]{:S(2)}) collective-permute-start(bf16[19,16,128]{2,1,0:T(8,128)(2,1)S(1)} %fusion.9), channel_id=1, source_target_pairs={{0,8},{4,12},{8,0},{12,4},{1,9},{5,13},{9,1},{13,5},{2,10},{6,14},... | collective-permute-start | bytes 233480 | tf_op jit(solution)/shard_map/ppermute | solution.py:536
  64.6 1.4 %collective-permute-start.7 = (f32[19,16,128]{2,1,0:T(8,128)S(1)}, f32[19,16,128]{2,1,0:T(8,128)S(1)}, u32[]{:S(2)}, u32[]{:S(2)}) collective-permute-start(f32[19,16,128]{2,1,0:T(8,128)S(1)} %fusion.7.mine_ref), channel_id=1, source_target_pairs={{0,1},{1,0},{2,3},{3,2},{4,5},{5,4},{6,7},{7,6},{8,9},{9,8},{10,11... | collective-permute-start | bytes 466952 | tf_op jit(solution)/shard_map/ppermute | solution.py:539
where the time goes:
time: 67.3 us; the launch traced here: 67.6 us
  starting transfers between devices  32.1 us (48%)
  Pallas kernels  15 us (22%)
  waiting for transfers between devices  14.6 us (22%)
  local copies, waits for them, and re-layouts  4.4 us (7%)
  between operations  0.85 us (1%)
    ppermute x1, starting transfers between devices, shards(): got = lax.ppermute(send, 'rep', swap)  12.9 us
    ppermute x3, starting transfers between devices, shards(): sent = lax.ppermute(wire[step].astype(BF16), ('bricks', 'chan'), routes)  11.5 us
    pallas_call x1, Pallas kernels, shards(): pl.pallas_call(main_kernel, out_shape=(parts, parts), in_specs=[smem] + [...  8.21 us
    pallas_call x1, Pallas kernels, shards(): pl.pallas_call(local_kernel, out_shape=(jax.ShapeDtypeStruct((slabs + 2,...  5.2 us
    ppermute x1, waiting for transfers between devices, shards(): pieces.append(lax.ppermute(packed, 'chan', ring))  4.33 us
    ppermute x1, waiting for transfers between devices, shards(): lax.ppermute(wire.astype(BF16), 'bricks', [(i, i ^ step) for i in range(b...  3.96 us
    ppermute x3, waiting for transfers between devices, shards(): sent = lax.ppermute(wire[step].astype(BF16), ('bricks', 'chan'), routes)  3.76 us
    ppermute x1, starting transfers between devices, shards(): lax.ppermute(wire.astype(BF16), 'bricks', [(i, i ^ step) for i in range(b...  3.18 us
  transfers between devices with their start and end apart: 8, of which 6 were waited for; matrix products, arithmetic and copies ran while one was open for 3% of the time, Pallas kernels for 8%

commit v1 on v0

--- a/solution.py
+++ b/solution.py
@@ -97,27 +97,20 @@
     )
 
 
-def pack_kernel(w1_ref, w2_ref, wd_ref, out_ref):
+def pack_kernel(w1_ref, w2_ref, wd_ref, first_ref, rest_ref):
     half = w1_ref.shape[1] // 2
-    start = 0
-    for ref in (w1_ref, w2_ref, wd_ref):
-        stop = start + ref.shape[0]
-        out_ref[start:stop] = jnp.concatenate([ref[:, :half], ref[:, half:]], axis=2)
-        start = stop
-
-
-def local_kernel(foot_ref, feat_ref, *refs):
+
+    def dense(ref):
+        return jnp.concatenate([ref[:, :half], ref[:, half:]], axis=2)
+
+    first_ref[...] = dense(w1_ref)
+    rest_ref[0 : w2_ref.shape[0]] = dense(w2_ref)
+    rest_ref[w2_ref.shape[0] :] = dense(wd_ref)
+
+
+def unpack(piece_refs, whole):
     chans = lax.axis_size("chan")
-    piece_refs = refs[:chans]
-    part_ref, y1_ref, m1_ref, m2_ref, down_ref, back_ref, whole, turned, arranged = refs[chans:-2]
-    even_window, odd_window = refs[-2:]
-    column = lax.axis_index("bricks") * lax.axis_size("rep") + lax.axis_index("rep")
     me = lax.axis_index("chan")
-    side = me * (BRICK // chans) // 4
-    count = 2 * foot_ref[1, column]
-    columns = lax.axis_size("bricks") * lax.axis_size("rep")
-    other_count, offset = neighbour(foot_ref, column, columns, side)
-
     half = piece_refs[0].shape[1]
     for step in range(chans):
         block = piece_refs[step][...]
@@ -126,18 +119,41 @@
             part = block[:, :, 64 * h : 64 * h + 64]
             rows = pl.ds(pl.multiple_of((2 * source + h) * half, half), half)
             whole[:, rows, :] = jnp.concatenate([part, part], axis=2)
-    for t in range(54):
+
+
+def turn_taps(whole, turned):
+    for t in range(27):
         turned[t] = jnp.concatenate([whole[t], whole[t]], axis=0).T[0:64]
-    build_conv(turned.at[0:27], m1_ref)
-    build_conv(turned.at[27:54], m2_ref)
+
+
+def mats_kernel(after_ref, *refs):
+    chans = lax.axis_size("chan")
+    m2_ref, down_ref, back_ref, whole, turned = refs[chans:]
+    unpack(refs[:chans], whole)
+    turn_taps(whole, turned)
+    build_conv(turned, m2_ref)
     low = lanes_low((64, 128))
     zero = jnp.zeros((64, 128), BF16)
     for t in range(8):
         ab, e = t // 2, t % 2
-        block = whole[54 + t]
+        block = whole[27 + t]
         tile = jnp.concatenate([jnp.where(low, block, zero), jnp.where(low, zero, block)], axis=0)
         down_ref[ab * 128 : ab * 128 + 128, e * 128 : e * 128 + 128] = tile
         back_ref[:, t * 128 : t * 128 + 128] = tile.T
+
+
+def local_kernel(foot_ref, feat_ref, *refs):
+    chans = lax.axis_size("chan")
+    part_ref, y1_ref, m1_ref, whole, turned, arranged, even_window, odd_window = refs[chans:]
+    column = lax.axis_index("bricks") * lax.axis_size("rep") + lax.axis_index("rep")
+    side = lax.axis_index("chan") * (BRICK // chans) // 4
+    count = 2 * foot_ref[1, column]
+    columns = lax.axis_size("bricks") * lax.axis_size("rep")
+    other_count, offset = neighbour(foot_ref, column, columns, side)
+
+    unpack(refs[:chans], whole)
+    turn_taps(whole, turned)
+    build_conv(turned, m1_ref)
 
     def turn(t, carry):
         for p in range(8):
@@ -441,18 +457,22 @@
     features = features[0]
     slabs = features.shape[2] // 4
 
-    packed = pl.pallas_call(
+    packs = pl.pallas_call(
         pack_kernel,
-        out_shape=jax.ShapeDtypeStruct((62, 32 // chans, 128), BF16),
+        out_shape=(
+            jax.ShapeDtypeStruct((27, 32 // chans, 128), BF16),
+            jax.ShapeDtypeStruct((35, 32 // chans, 128), BF16),
+        ),
         in_specs=[vmem] * 3,
-        out_specs=vmem,
+        out_specs=(vmem, vmem),
         compiler_params=pltpu.CompilerParams(vmem_limit_bytes=16 << 20),
         name="pack",
     )(w_first.transpose(0, 2, 1), w_second.transpose(0, 2, 1), w_down)
-    pieces = [packed]
-    for step in range(1, chans):
-        ring = [(i, (i + step) % chans) for i in range(chans)]
-        pieces.append(lax.ppermute(packed, "chan", ring))
+    pieces = [[packed] for packed in packs]
+    for packed, gathered in zip(packs, pieces):
+        for step in range(1, chans):
+            ring = [(i, (i + step) % chans) for i in range(chans)]
+            gathered.append(lax.ppermute(packed, "chan", ring))
 
     pairs = []
     for col in range(bricks * reps):
@@ -464,21 +484,18 @@
     outward = lax.dynamic_slice_in_dim(features, (1 - side) * 4, 4, 1).transpose(1, 2, 0, 3)
     halo = lax.ppermute(outward, ("bricks", "chan", "rep"), pairs)
 
-    part, near, mat1, mat2, down_mat, back_mat = pl.pallas_call(
+    part, near, mat1 = pl.pallas_call(
         local_kernel,
         out_shape=(
             jax.ShapeDtypeStruct((slabs + 2, 2 * ROWS, 256), F32),
             jax.ShapeDtypeStruct((4, slabs, ROWS, 128), BF16),
             jax.ShapeDtypeStruct((3, 1024, 256), BF16),
-            jax.ShapeDtypeStruct((3, 1024, 256), BF16),
-            jax.ShapeDtypeStruct((512, 256), BF16),
-            jax.ShapeDtypeStruct((128, 1024), BF16),
         ),
         in_specs=[smem] + [vmem] * (1 + chans),
-        out_specs=(vmem,) * 6,
+        out_specs=(vmem,) * 3,
         scratch_shapes=[
-            pltpu.VMEM((62, 64, 128), BF16),
-            pltpu.VMEM((54, 64, 128), BF16),
+            pltpu.VMEM((27, 64, 128), BF16),
+            pltpu.VMEM((27, 64, 128), BF16),
             pltpu.VMEM((8, slabs, ROWS, 128), BF16),
             pltpu.VMEM((8, ROWS, 256), BF16),
             pltpu.VMEM((8, ROWS, 256), BF16),
@@ -486,7 +503,20 @@
         compiler_params=pltpu.CompilerParams(vmem_limit_bytes=36 << 20),
         cost_estimate=pl.CostEstimate(flops=6 * 6 * 512 * 1024 * 512, bytes_accessed=8 << 20, transcendentals=0),
         name="first_local",
-    )(footprint, features.transpose(1, 2, 0, 3), *pieces)
+    )(footprint, features.transpose(1, 2, 0, 3), *pieces[0])
+    mat2, down_mat, back_mat = pl.pallas_call(
+        mats_kernel,
+        out_shape=(
+            jax.ShapeDtypeStruct((3, 1024, 256), BF16),
+            jax.ShapeDtypeStruct((512, 256), BF16),
+            jax.ShapeDtypeStruct((128, 1024), BF16),
+        ),
+        in_specs=[pl.BlockSpec(memory_space=pl.ANY)] + [vmem] * chans,
+        out_specs=(vmem,) * 3,
+        scratch_shapes=[pltpu.VMEM((35, 64, 128), BF16), pltpu.VMEM((27, 64, 128), BF16)],
+        compiler_params=pltpu.CompilerParams(vmem_limit_bytes=16 << 20),
+        name="mats",
+    )(near, *pieces[1])
     parts = jax.ShapeDtypeStruct((chans, 19, 64 // chans // reps, 128), F32)
     keep, send = pl.pallas_call(
         main_kernel,

time: 67.3 us -> 66.8 us (level); the launches traced: 67.6 us -> 66.1 us
  starting transfers between devices: 32.1 us -> 31 us
  waiting for transfers between devices: 14.6 us -> 13.9 us
    ppermute x1, starting transfers between devices: 12.9 us -> 22.2 us  [shards(): got = lax.ppermute(send, 'rep', swap)]
    ppermute x3, starting transfers between devices: 11.5 us -> 3.96 us  [shards(): sent = lax.ppermute(wire[step].astype(BF16), ('bricks', 'chan'), routes)]
    ppermute x1 -> x2, waiting for transfers between devices: 4.33 us -> 1.01 us  [shards(): gathered.append(lax.ppermute(packed, 'chan', ring))]
    ppermute x1, starting transfers between devices: 3.18 us -> 0.07 us  [shards(): lax.ppermute(wire.astype(BF16), 'bricks', [(i, i ^ step) for i in range(b...]
    ppermute x1, waiting for transfers between devices: 3.96 us -> 5.95 us  [shards(): lax.ppermute(wire.astype(BF16), 'bricks', [(i, i ^ step) for i in range(b...]
    ppermute x1 -> x2, starting transfers between devices: 1.84 us -> 2.09 us  [shards(): gathered.append(lax.ppermute(packed, 'chan', ring))]
  transfers between devices with their start and end apart: 8 -> 9, of which waited for: 6 -> 7; matrix products, arithmetic and copies ran while one was open for 3% -> 3% of each run, Pallas kernels for 8% -> 8%
where the time goes in v1:
time: 66.8 us; the launch traced here: 66.1 us
  starting transfers between devices  31 us (46%)
  Pallas kernels  15.3 us (23%)
  waiting for transfers between devices  13.9 us (21%)
  local copies, waits for them, and re-layouts  4.4 us (7%)
  between operations  0.88 us (1%)
    ppermute x1, starting transfers between devices, shards(): got = lax.ppermute(send, 'rep', swap)  22.2 us
    pallas_call x1, Pallas kernels, shards(): pl.pallas_call(main_kernel, out_shape=(parts, parts), in_specs=[smem] + [...  8.27 us
    ppermute x1, waiting for transfers between devices, shards(): lax.ppermute(wire.astype(BF16), 'bricks', [(i, i ^ step) for i in range(b...  5.95 us
    pallas_call x1, Pallas kernels, shards(): pl.pallas_call(local_kernel, out_shape=(jax.ShapeDtypeStruct((slabs + 2,...  4.76 us
    ppermute x3, waiting for transfers between devices, shards(): sent = lax.ppermute(wire[step].astype(BF16), ('bricks', 'chan'), routes)  4.39 us
    ppermute x3, starting transfers between devices, shards(): sent = lax.ppermute(wire[step].astype(BF16), ('bricks', 'chan'), routes)  3.96 us
    ppermute x1, starting transfers between devices, shards(): halo = lax.ppermute(outward, ('bricks', 'chan', 'rep'), pairs)  2.59 us
    dynamic_slice x2, local copies, waits for them, and re-layouts, shards(): lax.dynamic_slice_in_dim(features, (1 - side) * 4, 4, 1)  2.3 us
  transfers between devices with their start and end apart: 9, of which 7 were waited for; matrix products, arithmetic and copies ran while one was open for 3% of the time, Pallas kernels for 8%

profile of v1, /device:TPU:0, one launch (start us, length us, event | category | flops | bytes accessed | tf_op | source)
XLA Modules:
  0.0 66.1 jit_solution(12099074513809840551)
XLA Ops:
  0.6 1.7 %constant_dynamic-slice_fusion = bf16[1,64,4,24,128]{4,3,2,1,0:T(8,128)(2,1)S(1)} fusion(bf16[1,64,8,24,128]{4,3,2,1,0:T(8,128)(2,1)} %param.7, s32[]{:T(128)S(6)} %select_n.26), kind=kLoop, calls=%fused_computation.24 | loop fusion | bytes 3145732 | tf_op jit(solution)/shard_map/dynamic_slice | solution.py:484
  2.3 0.0 copy-start
  2.4 0.0 copy-start.1
  2.4 0.0 copy-start.2
  2.4 0.0 copy-start.6
  2.4 0.6 copy.16
  3.0 2.6 %collective-permute-start.1 = (bf16[4,24,64,128]{3,2,1,0:T(8,128)(2,1)S(1)}, bf16[4,24,64,128]{3,2,1,0:T(8,128)(2,1)S(1)}, u32[]{:S(2)}, u32[]{:S(2)}) collective-permute-start(bf16[4,24,64,128]{3,2,1,0:T(8,128)(2,1)S(1)} %bitcast.34), channel_id=1, source_target_pairs={{3,2},{0,1},{6,3},{1,4},{7,6},{4,5},{10,7},{5,8},{11,10},{8,9},{14... | collective-permute-start | bytes 4718600 | tf_op jit(solution)/shard_map/ppermute | solution.py:485
  5.6 0.0 copy-done
  5.6 0.0 copy-done.1
  5.6 0.0 copy-done.2
  5.6 0.1 pack.1
  5.8 1.8 %collective-permute-start = (bf16[27,16,128]{2,1,0:T(8,128)(2,1)S(1)}, bf16[27,16,128]{2,1,0:T(8,128)(2,1)S(1)}, u32[]{:S(2)}, u32[]{:S(2)}) collective-permute-start(bf16[27,16,128]{2,1,0:T(8,128)(2,1)S(1)} %get-tuple-element.18.refs_0_), channel_id=1, source_target_pairs={{0,2},{2,0},{1,3},{3,1},{4,6},{6,4},{5,7},{7,5},{8,10},{10,8},{9,1... | collective-permute-start | bytes 331784 | tf_op jit(solution)/shard_map/ppermute | solution.py:475
  7.6 0.0 copy-start.3
  7.6 0.3 collective-permute-start.2
  7.9 0.0 copy-done.6
  7.9 2.0 %copy.15 = bf16[1,64,8,24,128]{4,1,3,2,0:T(8,128)(2,1)S(1)} copy(bf16[1,64,8,24,128]{4,3,2,1,0:T(8,128)(2,1)S(1)} %copy-done.6) | data formatting | bytes 6291456 | tf_op args[0]
  9.9 1.0 %collective-permute-done.refs_1_ = bf16[27,16,128]{2,1,0:T(8,128)(2,1)S(1)} collective-permute-done((bf16[27,16,128]{2,1,0:T(8,128)(2,1)S(1)}, bf16[27,16,128]{2,1,0:T(8,128)(2,1)S(1)}, u32[]{:S(2)}, u32[]{:S(2)}) %collective-permute-start) | collective-permute-done | bytes 110624 | tf_op jit(solution)/shard_map/ppermute | solution.py:475
  10.9 0.0 copy-done.3
  10.9 4.8 %first_local.1 = (f32[8,512,256]{2,1,0:T(8,128)S(1)}, bf16[4,6,256,128]{3,2,1,0:T(8,128)(2,1)S(1)}, bf16[3,1024,256]{2,1,0:T(8,128)(2,1)S(1)}) custom-call(s32[2,8]{1,0:T(2,128)S(1)} %copy-done.3, bf16[8,24,64,128]{3,2,1,0:T(8,128)(2,1)S(1)} %bitcast.29, bf16[27,16,128]{2,1,0:T(8,128)(2,1)S(1)} %get-tuple-element.18.refs_0_, ...), custom_call_target="tpu_custom_call" | custom-call | flops 9663676416 | bytes 8388608 | tf_op jit(solution)/shard_map/first_local/pallas_call | solution.py:487
  15.7 0.0 copy-start.4
  15.7 0.0 copy-start.5
  15.7 0.0 collective-permute-done.2.refs_1_
  15.7 0.7 %mats.1 = (bf16[3,1024,256]{2,1,0:T(8,128)(2,1)S(1)}, bf16[512,256]{1,0:T(8,128)(2,1)S(1)}, bf16[128,1024]{1,0:T(8,128)(2,1)S(1)}) custom-call(bf16[4,6,256,128]{3,2,1,0:T(8,128)(2,1)S(1)} %get-tuple-element.20.after_ref.near_ref, bf16[35,16,128]{2,1,0:T(8,128)(2,1)S(1)} %get-tuple-element.22.refs_0_, bf16[35,16,128]{2,1,0:T(8,128)(2,1)S(1)} %collective-permute-done.2.refs_1_), custom_call_target="tpu_custom_call" | custom-call | tf_op jit(solution)/shard_map/mats/pallas_call | solution.py:507
  16.4 0.0 collective-permute-done.1.halo_ref
  16.4 0.0 copy-done.4
  16.4 0.0 copy-done.5
  16.4 8.3 %head_and_grads.1 = (f32[2,19,16,128]{3,2,1,0:T(8,128)S(1)}, f32[2,19,16,128]{3,2,1,0:T(8,128)S(1)}) custom-call(s32[2,8]{1,0:T(2,128)S(1)} %copy-done.3, f32[8,512,256]{2,1,0:T(8,128)S(1)} %get-tuple-element.19.part_ref, bf16[4,24,64,128]{3,2,1,0:T(8,128)(2,1)S(1)} %collective-permute-done.1.halo_ref, ...), custom_call_target="tpu_custom_call" | custom-call | flops 38654705664 | bytes 16777216 | tf_op jit(solution)/shard_map/head_and_grads/pallas_call | solution.py:521
  24.7 22.2 %collective-permute-start.3 = (f32[2,19,16,128]{3,2,1,0:T(8,128)S(1)}, f32[2,19,16,128]{3,2,1,0:T(8,128)S(1)}, u32[]{:S(2)}, u32[]{:S(2)}) collective-permute-start(f32[2,19,16,128]{3,2,1,0:T(8,128)S(1)} %get-tuple-element.27), channel_id=1, source_target_pairs={{0,1},{1,0},{2,3},{3,2},{4,5},{5,4},{6,7},{7,6},{8,9},{9,8},{10,11... | collective-permute-start | bytes 933896 | tf_op jit(solution)/shard_map/ppermute | solution.py:547
  46.9 1.2 %collective-permute-done.3 = f32[2,19,16,128]{3,2,1,0:T(8,128)S(1)} collective-permute-done((f32[2,19,16,128]{3,2,1,0:T(8,128)S(1)}, f32[2,19,16,128]{3,2,1,0:T(8,128)S(1)}, u32[]{:S(2)}, u32[]{:S(2)}) %collective-permute-start.3) | collective-permute-done | bytes 311328 | tf_op jit(solution)/shard_map/ppermute | solution.py:547
  48.1 0.1 fusion.8
  48.2 0.1 collective-permute-start.6
  48.3 3.9 %collective-permute-start.5 = (bf16[19,16,128]{2,1,0:T(8,128)(2,1)S(1)}, bf16[19,16,128]{2,1,0:T(8,128)(2,1)S(1)}, u32[]{:S(2)}, u32[]{:S(2)}) collective-permute-start(bf16[19,16,128]{2,1,0:T(8,128)(2,1)S(1)} %get-tuple-element.32), channel_id=1, source_target_pairs={{0,4},{2,6},{4,0},{6,2},{8,12},{10,14},{12,8},{14,10},{1,5},{3,7},... | collective-permute-start | bytes 233480 | tf_op jit(solution)/shard_map/ppermute | solution.py:560
  52.2 0.0 collective-permute-start.4
  52.2 2.2 %collective-permute-done.6 = bf16[19,16,128]{2,1,0:T(8,128)(2,1)S(1)} collective-permute-done((bf16[19,16,128]{2,1,0:T(8,128)(2,1)S(1)}, bf16[19,16,128]{2,1,0:T(8,128)(2,1)S(1)}, u32[]{:S(2)}, u32[]{:S(2)}) %collective-permute-start.6) | collective-permute-done | bytes 77856 | tf_op jit(solution)/shard_map/ppermute | solution.py:560
  54.4 2.1 %collective-permute-done.5 = bf16[19,16,128]{2,1,0:T(8,128)(2,1)S(1)} collective-permute-done((bf16[19,16,128]{2,1,0:T(8,128)(2,1)S(1)}, bf16[19,16,128]{2,1,0:T(8,128)(2,1)S(1)}, u32[]{:S(2)}, u32[]{:S(2)}) %collective-permute-start.5) | collective-permute-done | bytes 77856 | tf_op jit(solution)/shard_map/ppermute | solution.py:560
  56.5 0.1 collective-permute-done.4
  56.6 0.1 add_add_fusion
  56.8 0.1 fusion.9
  56.9 0.1 collective-permute-start.7
  57.0 6.0 %collective-permute-done.7 = bf16[19,16,128]{2,1,0:T(8,128)(2,1)S(1)} collective-permute-done((bf16[19,16,128]{2,1,0:T(8,128)(2,1)S(1)}, bf16[19,16,128]{2,1,0:T(8,128)(2,1)S(1)}, u32[]{:S(2)}, u32[]{:S(2)}) %collective-permute-start.7) | collective-permute-done | bytes 77856 | tf_op jit(solution)/shard_map/ppermute | solution.py:566
  62.9 0.1 convert_add_fusion
  63.1 0.1 fusion.7.mine_ref
  63.2 0.1 collective-permute-start.8
  63.2 1.4 %collective-permute-done.8.peer_ref = f32[19,16,128]{2,1,0:T(8,128)S(1)} collective-permute-done((f32[19,16,128]{2,1,0:T(8,128)S(1)}, f32[19,16,128]{2,1,0:T(8,128)S(1)}, u32[]{:S(2)}, u32[]{:S(2)}) %collective-permute-start.8) | collective-permute-done | bytes 155680 | tf_op jit(solution)/shard_map/ppermute | solution.py:569
  64.6 1.5 %assemble.1 = (f32[27,32,64]{2,1,0:T(8,128)}, f32[8,32,64]{2,1,0:T(8,128)}, f32[1,64]{1,0:T(1,128)}, f32[1,1]{1,0:T(1,128)}) custom-call(s32[2,8]{1,0:T(2,128)S(1)} %copy-done.3, f32[19,16,128]{2,1,0:T(8,128)S(1)} %fusion.7.mine_ref, f32[19,16,128]{2,1,0:T(8,128)S(1)} %collective-permute-done.8.peer_ref), custom_call_target="tpu_custom_call" | custom-call | tf_op jit(solution)/shard_map/assemble/pallas_call | solution.py:571
  (4 shorter events, 0.0 us)
Async XLA Ops:
  2.3 3.3 %copy-start = (bf16[27,64,32]{1,2,0:T(8,128)(2,1)S(1)}, bf16[27,64,32]{1,2,0:T(8,128)(2,1)}, u32[]{:S(2)}) copy-start(bf16[27,64,32]{1,2,0:T(8,128)(2,1)} %param.8) | copy-start | bytes 331780
  2.4 3.3 %copy-start.1 = (bf16[27,64,32]{1,2,0:T(8,128)(2,1)S(1)}, bf16[27,64,32]{1,2,0:T(8,128)(2,1)}, u32[]{:S(2)}) copy-start(bf16[27,64,32]{1,2,0:T(8,128)(2,1)} %param.9) | copy-start | bytes 331780
  2.4 3.3 %copy-start.2 = (bf16[8,32,64]{2,1,0:T(8,128)(2,1)S(1)}, bf16[8,32,64]{2,1,0:T(8,128)(2,1)}, u32[]{:S(2)}) copy-start(bf16[8,32,64]{2,1,0:T(8,128)(2,1)} %wd_ref.1) | copy-start | bytes 98308
  2.4 5.5 %copy-start.6 = (bf16[1,64,8,24,128]{4,3,2,1,0:T(8,128)(2,1)S(1)}, bf16[1,64,8,24,128]{4,3,2,1,0:T(8,128)(2,1)}, u32[]{:S(2)}) copy-start(bf16[1,64,8,24,128]{4,3,2,1,0:T(8,128)(2,1)} %param.7) | copy-start | bytes 9437188
  3.0 13.4 %collective-permute-start.1 = (bf16[4,24,64,128]{3,2,1,0:T(8,128)(2,1)S(1)}, bf16[4,24,64,128]{3,2,1,0:T(8,128)(2,1)S(1)}, u32[]{:S(2)}, u32[]{:S(2)}) collective-permute-start(bf16[4,24,64,128]{3,2,1,0:T(8,128)(2,1)S(1)} %bitcast.34), channel_id=1, source_target_pairs={{3,2},{0,1},{6,3},{1,4},{7,6},{4,5},{10,7},{5,8},{11,10},{8,9},{14... | collective-permute-start | bytes 4718600 | tf_op jit(solution)/shard_map/ppermute | solution.py:485
  5.8 5.1 %collective-permute-start = (bf16[27,16,128]{2,1,0:T(8,128)(2,1)S(1)}, bf16[27,16,128]{2,1,0:T(8,128)(2,1)S(1)}, u32[]{:S(2)}, u32[]{:S(2)}) collective-permute-start(bf16[27,16,128]{2,1,0:T(8,128)(2,1)S(1)} %get-tuple-element.18.refs_0_), channel_id=1, source_target_pairs={{0,2},{2,0},{1,3},{3,1},{4,6},{6,4},{5,7},{7,5},{8,10},{10,8},{9,1... | collective-permute-start | bytes 331784 | tf_op jit(solution)/shard_map/ppermute | solution.py:475
  7.6 3.3 %copy-start.3 = (s32[2,8]{1,0:T(2,128)S(1)}, s32[2,8]{1,0:T(2,128)}, u32[]{:S(2)}) copy-start(s32[2,8]{1,0:T(2,128)} %foot_ref.5) | copy-start | bytes 196
  7.6 8.1 %collective-permute-start.2 = (bf16[35,16,128]{2,1,0:T(8,128)(2,1)S(1)}, bf16[35,16,128]{2,1,0:T(8,128)(2,1)S(1)}, u32[]{:S(2)}, u32[]{:S(2)}) collective-permute-start(bf16[35,16,128]{2,1,0:T(8,128)(2,1)S(1)} %get-tuple-element.22.refs_0_), channel_id=1, source_target_pairs={{0,2},{2,0},{1,3},{3,1},{4,6},{6,4},{5,7},{7,5},{8,10},{10,8},{9,1... | collective-permute-start | bytes 430088 | tf_op jit(solution)/shard_map/ppermute | solution.py:475
  15.7 0.7 %copy-start.4 = (s32[1,4,768]{2,1,0:T(4,128)S(1)}, s32[1,4,768]{2,1,0:T(4,128)}, u32[]{:S(2)}) copy-start(s32[1,4,768]{2,1,0:T(4,128)} %param.13) | copy-start | bytes 36868
  15.7 0.7 %copy-start.5 = (f32[64]{0:T(128)S(1)}, f32[64]{0:T(128)}, u32[]{:S(2)}) copy-start(f32[64]{0:T(128)} %param.11) | copy-start | bytes 772
  24.7 23.4 %collective-permute-start.3 = (f32[2,19,16,128]{3,2,1,0:T(8,128)S(1)}, f32[2,19,16,128]{3,2,1,0:T(8,128)S(1)}, u32[]{:S(2)}, u32[]{:S(2)}) collective-permute-start(f32[2,19,16,128]{3,2,1,0:T(8,128)S(1)} %get-tuple-element.27), channel_id=1, source_target_pairs={{0,1},{1,0},{2,3},{3,2},{4,5},{5,4},{6,7},{7,6},{8,9},{9,8},{10,11... | collective-permute-start | bytes 933896 | tf_op jit(solution)/shard_map/ppermute | solution.py:547
  48.2 6.2 %collective-permute-start.6 = (bf16[19,16,128]{2,1,0:T(8,128)(2,1)S(1)}, bf16[19,16,128]{2,1,0:T(8,128)(2,1)S(1)}, u32[]{:S(2)}, u32[]{:S(2)}) collective-permute-start(bf16[19,16,128]{2,1,0:T(8,128)(2,1)S(1)} %get-tuple-element.33), channel_id=1, source_target_pairs={{0,6},{2,4},{4,2},{6,0},{8,14},{10,12},{12,10},{14,8},{1,7},{3,5},... | collective-permute-start | bytes 233480 | tf_op jit(solution)/shard_map/ppermute | solution.py:560
  48.3 8.1 %collective-permute-start.5 = (bf16[19,16,128]{2,1,0:T(8,128)(2,1)S(1)}, bf16[19,16,128]{2,1,0:T(8,128)(2,1)S(1)}, u32[]{:S(2)}, u32[]{:S(2)}) collective-permute-start(bf16[19,16,128]{2,1,0:T(8,128)(2,1)S(1)} %get-tuple-element.32), channel_id=1, source_target_pairs={{0,4},{2,6},{4,0},{6,2},{8,12},{10,14},{12,8},{14,10},{1,5},{3,7},... | collective-permute-start | bytes 233480 | tf_op jit(solution)/shard_map/ppermute | solution.py:560
  52.2 4.4 %collective-permute-start.4 = (bf16[19,16,128]{2,1,0:T(8,128)(2,1)S(1)}, bf16[19,16,128]{2,1,0:T(8,128)(2,1)S(1)}, u32[]{:S(2)}, u32[]{:S(2)}) collective-permute-start(bf16[19,16,128]{2,1,0:T(8,128)(2,1)S(1)} %get-tuple-element.33), channel_id=1, source_target_pairs={{0,2},{2,0},{4,6},{6,4},{8,10},{10,8},{12,14},{14,12},{1,3},{3,1},... | collective-permute-start | bytes 233480 | tf_op jit(solution)/shard_map/ppermute | solution.py:560
  56.9 6.0 %collective-permute-start.7 = (bf16[19,16,128]{2,1,0:T(8,128)(2,1)S(1)}, bf16[19,16,128]{2,1,0:T(8,128)(2,1)S(1)}, u32[]{:S(2)}, u32[]{:S(2)}) collective-permute-start(bf16[19,16,128]{2,1,0:T(8,128)(2,1)S(1)} %fusion.9), channel_id=1, source_target_pairs={{0,8},{4,12},{8,0},{12,4},{1,9},{5,13},{9,1},{13,5},{2,10},{6,14},... | collective-permute-start | bytes 233480 | tf_op jit(solution)/shard_map/ppermute | solution.py:566
  63.2 1.4 %collective-permute-start.8 = (f32[19,16,128]{2,1,0:T(8,128)S(1)}, f32[19,16,128]{2,1,0:T(8,128)S(1)}, u32[]{:S(2)}, u32[]{:S(2)}) collective-permute-start(f32[19,16,128]{2,1,0:T(8,128)S(1)} %fusion.7.mine_ref), channel_id=1, source_target_pairs={{0,1},{1,0},{2,3},{3,2},{4,5},{5,4},{6,7},{7,6},{8,9},{9,8},{10,11... | collective-permute-start | bytes 466952 | tf_op jit(solution)/shard_map/ppermute | solution.py:569

commit v2 on v1

--- a/solution.py
+++ b/solution.py
@@ -356,16 +356,22 @@
                 err = jnp.where(live, err, 0.0)
                 for n in range(4):
                     turned = err[128 * n : 128 * n + 128].astype(BF16).T
-                    col = n * 512 + a * 256 + b * 128
-                    err_t[128:256, col : col + 128] = turned
+                    row = 384 * (1 - n % 2)
+                    col = n // 2 * 512 + a * 256 + b * 128
+                    err_t[row + 128 : row + 256, col : col + 128] = turned
                     up = jnp.where(square_lane < 126, pltpu.roll(turned, 126, 1), jnp.zeros_like(turned))
                     down = jnp.where(square_lane >= 2, pltpu.roll(turned, 2, 1), jnp.zeros_like(turned))
-                    err_t[0:128, col : col + 128] = up
-                    err_t[256:384, col : col + 128] = down
+                    err_t[row : row + 128, col : col + 128] = up
+                    err_t[row + 256 : row + 384, col : col + 128] = down
         grad_down[...] += jnp.dot(delta_t[...], fine, preferred_element_type=F32)
-        for a in range(3):
-            rows = hwin[:, 2 * a : 2 * a + 4].reshape(8 * ROWS, 256)
-            grad[a] += jnp.dot(err_t[...], rows, preferred_element_type=F32)
+        for k in range(4):
+            rows = hwin[:, 2 * k : 2 * k + 2].reshape(4 * ROWS, 256)
+            lower, upper = (384, 768) if k == 0 else (0, 384) if k == 3 else (0, 768)
+            part = jnp.dot(err_t[lower:upper], rows, preferred_element_type=F32)
+            if k > 0:
+                grad[k - 1] += part[0:384]
+            if k < 3:
+                grad[k] += part[upper - lower - 384 :]
         return carry
 
     lax.fori_loop(0, count // 2, second, 0)
@@ -532,7 +538,7 @@
             pltpu.VMEM((384, 128), BF16),
             pltpu.VMEM((2, 2, 2, ROWS, 128), BF16),
             pltpu.VMEM((256, 512), BF16),
-            pltpu.VMEM((384, 2048), BF16),
+            pltpu.VMEM((768, 1024), BF16),
             pltpu.VMEM((3, 384, 256), F32),
             pltpu.VMEM((256, 512), F32),
             pltpu.VMEM((8, 128), F32),

time: 66.8 us -> 64.8 us (0.970); the launches traced: 66.1 us -> 64.8 us
  waiting for transfers between devices: 13.9 us -> 13.1 us
  Pallas kernels: 15.3 us -> 14.6 us
    pallas_call x1, Pallas kernels: 8.27 us -> 7.5 us  [shards(): pl.pallas_call(main_kernel, out_shape=(parts, parts), in_specs=[smem] + [...]
    ppermute x1, starting transfers between devices: 0.07 us -> 0.81 us  [shards(): lax.ppermute(wire.astype(BF16), 'bricks', [(i, i ^ step) for i in range(b...]
    ppermute x3, waiting for transfers between devices: 4.39 us -> 3.7 us  [shards(): sent = lax.ppermute(wire[step].astype(BF16), ('bricks', 'chan'), routes)]
  transfers between devices with their start and end apart: 9 -> 9, of which waited for: 7 -> 6; matrix products, arithmetic and copies ran while one was open for 3% -> 3% of each run, Pallas kernels for 8% -> 9%
where the time goes in v2:
time: 64.8 us
  starting transfers between devices  31.3 us (48%)
  Pallas kernels  14.6 us (23%)
  waiting for transfers between devices  13.1 us (20%)
  local copies, waits for them, and re-layouts  4.4 us (7%)
  between operations  0.87 us (1%)
    ppermute x1, starting transfers between devices, shards(): got = lax.ppermute(send, 'rep', swap)  22.2 us
    pallas_call x1, Pallas kernels, shards(): pl.pallas_call(main_kernel, out_shape=(parts, parts), in_specs=[smem] + [...  7.5 us
    ppermute x1, waiting for transfers between devices, shards(): lax.ppermute(wire.astype(BF16), 'bricks', [(i, i ^ step) for i in range(b...  5.78 us
    pallas_call x1, Pallas kernels, shards(): pl.pallas_call(local_kernel, out_shape=(jax.ShapeDtypeStruct((slabs + 2,...  4.76 us
    ppermute x3, waiting for transfers between devices, shards(): sent = lax.ppermute(wire[step].astype(BF16), ('bricks', 'chan'), routes)  3.7 us
    ppermute x3, starting transfers between devices, shards(): sent = lax.ppermute(wire[step].astype(BF16), ('bricks', 'chan'), routes)  3.56 us
    ppermute x1, starting transfers between devices, shards(): halo = lax.ppermute(outward, ('bricks', 'chan', 'rep'), pairs)  2.59 us
    dynamic_slice x2, local copies, waits for them, and re-layouts, shards(): lax.dynamic_slice_in_dim(features, (1 - side) * 4, 4, 1)  2.3 us
  transfers between devices with their start and end apart: 9, of which 6 were waited for; matrix products, arithmetic and copies ran while one was open for 3% of the time, Pallas kernels for 9%

profile of v2, /device:TPU:0, one launch (start us, length us, event | category | flops | bytes accessed | tf_op | source)
XLA Modules:
  0.0 64.8 jit_solution(534663189116497439)
XLA Ops:
  0.6 1.7 %constant_dynamic-slice_fusion = bf16[1,64,4,24,128]{4,3,2,1,0:T(8,128)(2,1)S(1)} fusion(bf16[1,64,8,24,128]{4,3,2,1,0:T(8,128)(2,1)} %param.7, s32[]{:T(128)S(6)} %select_n.26), kind=kLoop, calls=%fused_computation.24 | loop fusion | bytes 3145732 | tf_op jit(solution)/shard_map/dynamic_slice | solution.py:490
  2.3 0.0 copy-start
  2.4 0.0 copy-start.1
  2.4 0.0 copy-start.2
  2.4 0.0 copy-start.6
  2.4 0.6 copy.16
  3.0 2.6 %collective-permute-start.1 = (bf16[4,24,64,128]{3,2,1,0:T(8,128)(2,1)S(1)}, bf16[4,24,64,128]{3,2,1,0:T(8,128)(2,1)S(1)}, u32[]{:S(2)}, u32[]{:S(2)}) collective-permute-start(bf16[4,24,64,128]{3,2,1,0:T(8,128)(2,1)S(1)} %bitcast.34), channel_id=1, source_target_pairs={{3,2},{0,1},{6,3},{1,4},{7,6},{4,5},{10,7},{5,8},{11,10},{8,9},{14... | collective-permute-start | bytes 4718600 | tf_op jit(solution)/shard_map/ppermute | solution.py:491
  5.6 0.0 copy-done
  5.6 0.0 copy-done.1
  5.6 0.0 copy-done.2
  5.6 0.1 pack.1
  5.8 1.8 %collective-permute-start = (bf16[27,16,128]{2,1,0:T(8,128)(2,1)S(1)}, bf16[27,16,128]{2,1,0:T(8,128)(2,1)S(1)}, u32[]{:S(2)}, u32[]{:S(2)}) collective-permute-start(bf16[27,16,128]{2,1,0:T(8,128)(2,1)S(1)} %get-tuple-element.18.refs_0_), channel_id=1, source_target_pairs={{0,2},{2,0},{1,3},{3,1},{4,6},{6,4},{5,7},{7,5},{8,10},{10,8},{9,1... | collective-permute-start | bytes 331784 | tf_op jit(solution)/shard_map/ppermute | solution.py:481
  7.6 0.0 copy-start.3
  7.6 0.3 collective-permute-start.2
  7.9 0.0 copy-done.6
  7.9 2.0 %copy.15 = bf16[1,64,8,24,128]{4,1,3,2,0:T(8,128)(2,1)S(1)} copy(bf16[1,64,8,24,128]{4,3,2,1,0:T(8,128)(2,1)S(1)} %copy-done.6) | data formatting | bytes 6291456 | tf_op args[0]
  9.9 1.0 %collective-permute-done.refs_1_ = bf16[27,16,128]{2,1,0:T(8,128)(2,1)S(1)} collective-permute-done((bf16[27,16,128]{2,1,0:T(8,128)(2,1)S(1)}, bf16[27,16,128]{2,1,0:T(8,128)(2,1)S(1)}, u32[]{:S(2)}, u32[]{:S(2)}) %collective-permute-start) | collective-permute-done | bytes 110624 | tf_op jit(solution)/shard_map/ppermute | solution.py:481
  10.9 0.0 copy-done.3
  10.9 4.8 %first_local.1 = (f32[8,512,256]{2,1,0:T(8,128)S(1)}, bf16[4,6,256,128]{3,2,1,0:T(8,128)(2,1)S(1)}, bf16[3,1024,256]{2,1,0:T(8,128)(2,1)S(1)}) custom-call(s32[2,8]{1,0:T(2,128)S(1)} %copy-done.3, bf16[8,24,64,128]{3,2,1,0:T(8,128)(2,1)S(1)} %bitcast.29, bf16[27,16,128]{2,1,0:T(8,128)(2,1)S(1)} %get-tuple-element.18.refs_0_, ...), custom_call_target="tpu_custom_call" | custom-call | flops 9663676416 | bytes 8388608 | tf_op jit(solution)/shard_map/first_local/pallas_call | solution.py:493
  15.7 0.0 copy-start.4
  15.7 0.0 copy-start.5
  15.7 0.0 collective-permute-done.2.refs_1_
  15.7 0.7 %mats.1 = (bf16[3,1024,256]{2,1,0:T(8,128)(2,1)S(1)}, bf16[512,256]{1,0:T(8,128)(2,1)S(1)}, bf16[128,1024]{1,0:T(8,128)(2,1)S(1)}) custom-call(bf16[4,6,256,128]{3,2,1,0:T(8,128)(2,1)S(1)} %get-tuple-element.20.after_ref.near_ref, bf16[35,16,128]{2,1,0:T(8,128)(2,1)S(1)} %get-tuple-element.22.refs_0_, bf16[35,16,128]{2,1,0:T(8,128)(2,1)S(1)} %collective-permute-done.2.refs_1_), custom_call_target="tpu_custom_call" | custom-call | tf_op jit(solution)/shard_map/mats/pallas_call | solution.py:513
  16.4 0.0 collective-permute-done.1.halo_ref
  16.4 0.0 copy-done.4
  16.4 0.0 copy-done.5
  16.4 7.5 %head_and_grads.1 = (f32[2,19,16,128]{3,2,1,0:T(8,128)S(1)}, f32[2,19,16,128]{3,2,1,0:T(8,128)S(1)}) custom-call(s32[2,8]{1,0:T(2,128)S(1)} %copy-done.3, f32[8,512,256]{2,1,0:T(8,128)S(1)} %get-tuple-element.19.part_ref, bf16[4,24,64,128]{3,2,1,0:T(8,128)(2,1)S(1)} %collective-permute-done.1.halo_ref, ...), custom_call_target="tpu_custom_call" | custom-call | flops 38654705664 | bytes 16777216 | tf_op jit(solution)/shard_map/head_and_grads/pallas_call | solution.py:527
  23.9 22.2 %collective-permute-start.3 = (f32[2,19,16,128]{3,2,1,0:T(8,128)S(1)}, f32[2,19,16,128]{3,2,1,0:T(8,128)S(1)}, u32[]{:S(2)}, u32[]{:S(2)}) collective-permute-start(f32[2,19,16,128]{3,2,1,0:T(8,128)S(1)} %get-tuple-element.27), channel_id=1, source_target_pairs={{0,1},{1,0},{2,3},{3,2},{4,5},{5,4},{6,7},{7,6},{8,9},{9,8},{10,11... | collective-permute-start | bytes 933896 | tf_op jit(solution)/shard_map/ppermute | solution.py:553
  46.2 1.2 %collective-permute-done.3 = f32[2,19,16,128]{3,2,1,0:T(8,128)S(1)} collective-permute-done((f32[2,19,16,128]{3,2,1,0:T(8,128)S(1)}, f32[2,19,16,128]{3,2,1,0:T(8,128)S(1)}, u32[]{:S(2)}, u32[]{:S(2)}) %collective-permute-start.3) | collective-permute-done | bytes 311328 | tf_op jit(solution)/shard_map/ppermute | solution.py:553
  47.4 0.1 fusion.8
  47.5 0.1 collective-permute-start.6
  47.6 1.8 %collective-permute-start.5 = (bf16[19,16,128]{2,1,0:T(8,128)(2,1)S(1)}, bf16[19,16,128]{2,1,0:T(8,128)(2,1)S(1)}, u32[]{:S(2)}, u32[]{:S(2)}) collective-permute-start(bf16[19,16,128]{2,1,0:T(8,128)(2,1)S(1)} %get-tuple-element.32), channel_id=1, source_target_pairs={{0,4},{2,6},{4,0},{6,2},{8,12},{10,14},{12,8},{14,10},{1,5},{3,7},... | collective-permute-start | bytes 233480 | tf_op jit(solution)/shard_map/ppermute | solution.py:566
  49.4 1.6 %collective-permute-start.4 = (bf16[19,16,128]{2,1,0:T(8,128)(2,1)S(1)}, bf16[19,16,128]{2,1,0:T(8,128)(2,1)S(1)}, u32[]{:S(2)}, u32[]{:S(2)}) collective-permute-start(bf16[19,16,128]{2,1,0:T(8,128)(2,1)S(1)} %get-tuple-element.33), channel_id=1, source_target_pairs={{0,2},{2,0},{4,6},{6,4},{8,10},{10,8},{12,14},{14,12},{1,3},{3,1},... | collective-permute-start | bytes 233480 | tf_op jit(solution)/shard_map/ppermute | solution.py:566
  51.1 2.6 %collective-permute-done.6 = bf16[19,16,128]{2,1,0:T(8,128)(2,1)S(1)} collective-permute-done((bf16[19,16,128]{2,1,0:T(8,128)(2,1)S(1)}, bf16[19,16,128]{2,1,0:T(8,128)(2,1)S(1)}, u32[]{:S(2)}, u32[]{:S(2)}) %collective-permute-start.6) | collective-permute-done | bytes 77856 | tf_op jit(solution)/shard_map/ppermute | solution.py:566
  53.6 0.0 collective-permute-done.5
  53.7 1.1 %collective-permute-done.4 = bf16[19,16,128]{2,1,0:T(8,128)(2,1)S(1)} collective-permute-done((bf16[19,16,128]{2,1,0:T(8,128)(2,1)S(1)}, bf16[19,16,128]{2,1,0:T(8,128)(2,1)S(1)}, u32[]{:S(2)}, u32[]{:S(2)}) %collective-permute-start.4) | collective-permute-done | bytes 77856 | tf_op jit(solution)/shard_map/ppermute | solution.py:566
  54.8 0.1 add_add_fusion
  54.9 0.1 fusion.9
  55.0 0.8 %collective-permute-start.7 = (bf16[19,16,128]{2,1,0:T(8,128)(2,1)S(1)}, bf16[19,16,128]{2,1,0:T(8,128)(2,1)S(1)}, u32[]{:S(2)}, u32[]{:S(2)}) collective-permute-start(bf16[19,16,128]{2,1,0:T(8,128)(2,1)S(1)} %fusion.9), channel_id=1, source_target_pairs={{0,8},{4,12},{8,0},{12,4},{1,9},{5,13},{9,1},{13,5},{2,10},{6,14},... | collective-permute-start | bytes 233480 | tf_op jit(solution)/shard_map/ppermute | solution.py:572
  55.8 5.8 %collective-permute-done.7 = bf16[19,16,128]{2,1,0:T(8,128)(2,1)S(1)} collective-permute-done((bf16[19,16,128]{2,1,0:T(8,128)(2,1)S(1)}, bf16[19,16,128]{2,1,0:T(8,128)(2,1)S(1)}, u32[]{:S(2)}, u32[]{:S(2)}) %collective-permute-start.7) | collective-permute-done | bytes 77856 | tf_op jit(solution)/shard_map/ppermute | solution.py:572
  61.6 0.1 convert_add_fusion
  61.8 0.1 fusion.7.mine_ref
  61.9 0.1 collective-permute-start.8
  62.0 1.4 %collective-permute-done.8.peer_ref = f32[19,16,128]{2,1,0:T(8,128)S(1)} collective-permute-done((f32[19,16,128]{2,1,0:T(8,128)S(1)}, f32[19,16,128]{2,1,0:T(8,128)S(1)}, u32[]{:S(2)}, u32[]{:S(2)}) %collective-permute-start.8) | collective-permute-done | bytes 155680 | tf_op jit(solution)/shard_map/ppermute | solution.py:575
  63.3 1.5 %assemble.1 = (f32[27,32,64]{2,1,0:T(8,128)}, f32[8,32,64]{2,1,0:T(8,128)}, f32[1,64]{1,0:T(1,128)}, f32[1,1]{1,0:T(1,128)}) custom-call(s32[2,8]{1,0:T(2,128)S(1)} %copy-done.3, f32[19,16,128]{2,1,0:T(8,128)S(1)} %fusion.7.mine_ref, f32[19,16,128]{2,1,0:T(8,128)S(1)} %collective-permute-done.8.peer_ref), custom_call_target="tpu_custom_call" | custom-call | tf_op jit(solution)/shard_map/assemble/pallas_call | solution.py:577
  (4 shorter events, 0.0 us)
Async XLA Ops:
  2.3 3.3 %copy-start = (bf16[27,64,32]{1,2,0:T(8,128)(2,1)S(1)}, bf16[27,64,32]{1,2,0:T(8,128)(2,1)}, u32[]{:S(2)}) copy-start(bf16[27,64,32]{1,2,0:T(8,128)(2,1)} %param.8) | copy-start | bytes 331780
  2.4 3.3 %copy-start.1 = (bf16[27,64,32]{1,2,0:T(8,128)(2,1)S(1)}, bf16[27,64,32]{1,2,0:T(8,128)(2,1)}, u32[]{:S(2)}) copy-start(bf16[27,64,32]{1,2,0:T(8,128)(2,1)} %param.9) | copy-start | bytes 331780
  2.4 3.3 %copy-start.2 = (bf16[8,32,64]{2,1,0:T(8,128)(2,1)S(1)}, bf16[8,32,64]{2,1,0:T(8,128)(2,1)}, u32[]{:S(2)}) copy-start(bf16[8,32,64]{2,1,0:T(8,128)(2,1)} %wd_ref.1) | copy-start | bytes 98308
  2.4 5.5 %copy-start.6 = (bf16[1,64,8,24,128]{4,3,2,1,0:T(8,128)(2,1)S(1)}, bf16[1,64,8,24,128]{4,3,2,1,0:T(8,128)(2,1)}, u32[]{:S(2)}) copy-start(bf16[1,64,8,24,128]{4,3,2,1,0:T(8,128)(2,1)} %param.7) | copy-start | bytes 9437188
  3.0 13.4 %collective-permute-start.1 = (bf16[4,24,64,128]{3,2,1,0:T(8,128)(2,1)S(1)}, bf16[4,24,64,128]{3,2,1,0:T(8,128)(2,1)S(1)}, u32[]{:S(2)}, u32[]{:S(2)}) collective-permute-start(bf16[4,24,64,128]{3,2,1,0:T(8,128)(2,1)S(1)} %bitcast.34), channel_id=1, source_target_pairs={{3,2},{0,1},{6,3},{1,4},{7,6},{4,5},{10,7},{5,8},{11,10},{8,9},{14... | collective-permute-start | bytes 4718600 | tf_op jit(solution)/shard_map/ppermute | solution.py:491
  5.8 5.1 %collective-permute-start = (bf16[27,16,128]{2,1,0:T(8,128)(2,1)S(1)}, bf16[27,16,128]{2,1,0:T(8,128)(2,1)S(1)}, u32[]{:S(2)}, u32[]{:S(2)}) collective-permute-start(bf16[27,16,128]{2,1,0:T(8,128)(2,1)S(1)} %get-tuple-element.18.refs_0_), channel_id=1, source_target_pairs={{0,2},{2,0},{1,3},{3,1},{4,6},{6,4},{5,7},{7,5},{8,10},{10,8},{9,1... | collective-permute-start | bytes 331784 | tf_op jit(solution)/shard_map/ppermute | solution.py:481
  7.6 3.3 %copy-start.3 = (s32[2,8]{1,0:T(2,128)S(1)}, s32[2,8]{1,0:T(2,128)}, u32[]{:S(2)}) copy-start(s32[2,8]{1,0:T(2,128)} %foot_ref.5) | copy-start | bytes 196
  7.6 8.1 %collective-permute-start.2 = (bf16[35,16,128]{2,1,0:T(8,128)(2,1)S(1)}, bf16[35,16,128]{2,1,0:T(8,128)(2,1)S(1)}, u32[]{:S(2)}, u32[]{:S(2)}) collective-permute-start(bf16[35,16,128]{2,1,0:T(8,128)(2,1)S(1)} %get-tuple-element.22.refs_0_), channel_id=1, source_target_pairs={{0,2},{2,0},{1,3},{3,1},{4,6},{6,4},{5,7},{7,5},{8,10},{10,8},{9,1... | collective-permute-start | bytes 430088 | tf_op jit(solution)/shard_map/ppermute | solution.py:481
  15.7 0.7 %copy-start.4 = (s32[1,4,768]{2,1,0:T(4,128)S(1)}, s32[1,4,768]{2,1,0:T(4,128)}, u32[]{:S(2)}) copy-start(s32[1,4,768]{2,1,0:T(4,128)} %param.13) | copy-start | bytes 36868
  15.7 0.7 %copy-start.5 = (f32[64]{0:T(128)S(1)}, f32[64]{0:T(128)}, u32[]{:S(2)}) copy-start(f32[64]{0:T(128)} %param.11) | copy-start | bytes 772
  23.9 23.4 %collective-permute-start.3 = (f32[2,19,16,128]{3,2,1,0:T(8,128)S(1)}, f32[2,19,16,128]{3,2,1,0:T(8,128)S(1)}, u32[]{:S(2)}, u32[]{:S(2)}) collective-permute-start(f32[2,19,16,128]{3,2,1,0:T(8,128)S(1)} %get-tuple-element.27), channel_id=1, source_target_pairs={{0,1},{1,0},{2,3},{3,2},{4,5},{5,4},{6,7},{7,6},{8,9},{9,8},{10,11... | collective-permute-start | bytes 933896 | tf_op jit(solution)/shard_map/ppermute | solution.py:553
  47.5 6.2 %collective-permute-start.6 = (bf16[19,16,128]{2,1,0:T(8,128)(2,1)S(1)}, bf16[19,16,128]{2,1,0:T(8,128)(2,1)S(1)}, u32[]{:S(2)}, u32[]{:S(2)}) collective-permute-start(bf16[19,16,128]{2,1,0:T(8,128)(2,1)S(1)} %get-tuple-element.33), channel_id=1, source_target_pairs={{0,6},{2,4},{4,2},{6,0},{8,14},{10,12},{12,10},{14,8},{1,7},{3,5},... | collective-permute-start | bytes 233480 | tf_op jit(solution)/shard_map/ppermute | solution.py:566
  47.6 6.1 %collective-permute-start.5 = (bf16[19,16,128]{2,1,0:T(8,128)(2,1)S(1)}, bf16[19,16,128]{2,1,0:T(8,128)(2,1)S(1)}, u32[]{:S(2)}, u32[]{:S(2)}) collective-permute-start(bf16[19,16,128]{2,1,0:T(8,128)(2,1)S(1)} %get-tuple-element.32), channel_id=1, source_target_pairs={{0,4},{2,6},{4,0},{6,2},{8,12},{10,14},{12,8},{14,10},{1,5},{3,7},... | collective-permute-start | bytes 233480 | tf_op jit(solution)/shard_map/ppermute | solution.py:566
  49.4 5.3 %collective-permute-start.4 = (bf16[19,16,128]{2,1,0:T(8,128)(2,1)S(1)}, bf16[19,16,128]{2,1,0:T(8,128)(2,1)S(1)}, u32[]{:S(2)}, u32[]{:S(2)}) collective-permute-start(bf16[19,16,128]{2,1,0:T(8,128)(2,1)S(1)} %get-tuple-element.33), channel_id=1, source_target_pairs={{0,2},{2,0},{4,6},{6,4},{8,10},{10,8},{12,14},{14,12},{1,3},{3,1},... | collective-permute-start | bytes 233480 | tf_op jit(solution)/shard_map/ppermute | solution.py:566
  55.0 6.6 %collective-permute-start.7 = (bf16[19,16,128]{2,1,0:T(8,128)(2,1)S(1)}, bf16[19,16,128]{2,1,0:T(8,128)(2,1)S(1)}, u32[]{:S(2)}, u32[]{:S(2)}) collective-permute-start(bf16[19,16,128]{2,1,0:T(8,128)(2,1)S(1)} %fusion.9), channel_id=1, source_target_pairs={{0,8},{4,12},{8,0},{12,4},{1,9},{5,13},{9,1},{13,5},{2,10},{6,14},... | collective-permute-start | bytes 233480 | tf_op jit(solution)/shard_map/ppermute | solution.py:572
  61.9 1.4 %collective-permute-start.8 = (f32[19,16,128]{2,1,0:T(8,128)S(1)}, f32[19,16,128]{2,1,0:T(8,128)S(1)}, u32[]{:S(2)}, u32[]{:S(2)}) collective-permute-start(f32[19,16,128]{2,1,0:T(8,128)S(1)} %fusion.7.mine_ref), channel_id=1, source_target_pairs={{0,1},{1,0},{2,3},{3,2},{4,5},{5,4},{6,7},{7,6},{8,9},{9,8},{10,11... | collective-permute-start | bytes 466952 | tf_op jit(solution)/shard_map/ppermute | solution.py:575

commit v3 on v2

--- a/solution.py
+++ b/solution.py
@@ -186,7 +186,8 @@
         return carry
 
     def beside(t):
-        fill(even_window, t)
+        for p in range(4):
+            fill_window(even_window, 4 * side + p, arranged, 4 * side + p, t, count)
         edge(even_window, t)
 
     rims(count, offset, other_count, beside)

time: 64.8 us -> 64.1 us (0.989)
  starting transfers between devices: 31.3 us -> 12.1 us
  Pallas kernels: 14.6 us -> 32.5 us
    ppermute x1, starting transfers between devices: 22.2 us -> 0.07 us  [shards(): got = lax.ppermute(send, 'rep', swap)]
    pallas_call x1, Pallas kernels: 7.5 us -> 18.7 us  [shards(): pl.pallas_call(main_kernel, out_shape=(parts, parts), in_specs=[smem] + [...]
    pallas_call x1, Pallas kernels: 4.76 us -> 11.5 us  [shards(): pl.pallas_call(local_kernel, out_shape=(jax.ShapeDtypeStruct((slabs + 2,...]
    ppermute x3, starting transfers between devices: 3.56 us -> 7.18 us  [shards(): sent = lax.ppermute(wire[step].astype(BF16), ('bricks', 'chan'), routes)]
    ppermute x1, starting transfers between devices: 0.81 us -> 0.07 us  [shards(): lax.ppermute(wire.astype(BF16), 'bricks', [(i, i ^ step) for i in range(b...]
  transfers between devices with their start and end apart: 9 -> 9, of which waited for: 6 -> 6; matrix products, arithmetic and copies ran while one was open for 3% -> 3% of each run, Pallas kernels for 9% -> 19%
where the time goes in v3:
time: 64.1 us; the launch traced here: 63.5 us
  Pallas kernels  32.5 us (51%)
  waiting for transfers between devices  13.1 us (20%)
  starting transfers between devices  12.1 us (19%)
  local copies, waits for them, and re-layouts  4.4 us (7%)
  between operations  0.89 us (1%)
    pallas_call x1, Pallas kernels, shards(): pl.pallas_call(main_kernel, out_shape=(parts, parts), in_specs=[smem] + [...  18.7 us
    pallas_call x1, Pallas kernels, shards(): pl.pallas_call(local_kernel, out_shape=(jax.ShapeDtypeStruct((slabs + 2,...  11.5 us
    ppermute x3, starting transfers between devices, shards(): sent = lax.ppermute(wire[step].astype(BF16), ('bricks', 'chan'), routes)  7.18 us
    ppermute x1, waiting for transfers between devices, shards(): lax.ppermute(wire.astype(BF16), 'bricks', [(i, i ^ step) for i in range(b...  6.12 us
    ppermute x3, waiting for transfers between devices, shards(): sent = lax.ppermute(wire[step].astype(BF16), ('bricks', 'chan'), routes)  3.08 us
    ppermute x1, starting transfers between devices, shards(): halo = lax.ppermute(outward, ('bricks', 'chan', 'rep'), pairs)  2.59 us
    dynamic_slice x2, local copies, waits for them, and re-layouts, shards(): lax.dynamic_slice_in_dim(features, (1 - side) * 4, 4, 1)  2.3 us
    ppermute x2, starting transfers between devices, shards(): gathered.append(lax.ppermute(packed, 'chan', ring))  2.09 us
  transfers between devices with their start and end apart: 9, of which 6 were waited for; matrix products, arithmetic and copies ran while one was open for 3% of the time, Pallas kernels for 19%

profile of v3, /device:TPU:0, one launch (start us, length us, event | category | flops | bytes accessed | tf_op | source)
XLA Modules:
  0.0 63.5 jit_solution(7858946882829546629)
XLA Ops:
  0.6 1.7 %constant_dynamic-slice_fusion = bf16[1,64,4,24,128]{4,3,2,1,0:T(8,128)(2,1)S(1)} fusion(bf16[1,64,8,24,128]{4,3,2,1,0:T(8,128)(2,1)} %param.7, s32[]{:T(128)S(6)} %select_n.26), kind=kLoop, calls=%fused_computation.24 | loop fusion | bytes 3145732 | tf_op jit(solution)/shard_map/dynamic_slice | solution.py:491
  2.3 0.0 copy-start
  2.4 0.0 copy-start.1
  2.4 0.0 copy-start.2
  2.4 0.0 copy-start.6
  2.4 0.6 copy.16
  3.0 2.6 %collective-permute-start.1 = (bf16[4,24,64,128]{3,2,1,0:T(8,128)(2,1)S(1)}, bf16[4,24,64,128]{3,2,1,0:T(8,128)(2,1)S(1)}, u32[]{:S(2)}, u32[]{:S(2)}) collective-permute-start(bf16[4,24,64,128]{3,2,1,0:T(8,128)(2,1)S(1)} %bitcast.34), channel_id=1, source_target_pairs={{3,2},{0,1},{6,3},{1,4},{7,6},{4,5},{10,7},{5,8},{11,10},{8,9},{14... | collective-permute-start | bytes 4718600 | tf_op jit(solution)/shard_map/ppermute | solution.py:492
  5.6 0.0 copy-done
  5.6 0.0 copy-done.1
  5.6 0.0 copy-done.2
  5.6 0.1 pack.1
  5.8 1.8 %collective-permute-start = (bf16[27,16,128]{2,1,0:T(8,128)(2,1)S(1)}, bf16[27,16,128]{2,1,0:T(8,128)(2,1)S(1)}, u32[]{:S(2)}, u32[]{:S(2)}) collective-permute-start(bf16[27,16,128]{2,1,0:T(8,128)(2,1)S(1)} %get-tuple-element.18.refs_0_), channel_id=1, source_target_pairs={{0,2},{2,0},{1,3},{3,1},{4,6},{6,4},{5,7},{7,5},{8,10},{10,8},{9,1... | collective-permute-start | bytes 331784 | tf_op jit(solution)/shard_map/ppermute | solution.py:482
  7.6 0.0 copy-start.3
  7.6 0.3 collective-permute-start.2
  7.9 0.0 copy-done.6
  7.9 2.0 %copy.15 = bf16[1,64,8,24,128]{4,1,3,2,0:T(8,128)(2,1)S(1)} copy(bf16[1,64,8,24,128]{4,3,2,1,0:T(8,128)(2,1)S(1)} %copy-done.6) | data formatting | bytes 6291456 | tf_op args[0]
  9.9 1.0 %collective-permute-done.refs_1_ = bf16[27,16,128]{2,1,0:T(8,128)(2,1)S(1)} collective-permute-done((bf16[27,16,128]{2,1,0:T(8,128)(2,1)S(1)}, bf16[27,16,128]{2,1,0:T(8,128)(2,1)S(1)}, u32[]{:S(2)}, u32[]{:S(2)}) %collective-permute-start) | collective-permute-done | bytes 110624 | tf_op jit(solution)/shard_map/ppermute | solution.py:482
  10.9 0.0 copy-done.3
  10.9 11.5 %first_local.1 = (f32[8,512,256]{2,1,0:T(8,128)S(1)}, bf16[4,6,256,128]{3,2,1,0:T(8,128)(2,1)S(1)}, bf16[3,1024,256]{2,1,0:T(8,128)(2,1)S(1)}) custom-call(s32[2,8]{1,0:T(2,128)S(1)} %copy-done.3, bf16[8,24,64,128]{3,2,1,0:T(8,128)(2,1)S(1)} %bitcast.29, bf16[27,16,128]{2,1,0:T(8,128)(2,1)S(1)} %get-tuple-element.18.refs_0_, ...), custom_call_target="tpu_custom_call" | custom-call | flops 9663676416 | bytes 8388608 | tf_op jit(solution)/shard_map/first_local/pallas_call | solution.py:494
  22.4 0.0 copy-start.4
  22.4 0.0 copy-start.5
  22.4 0.0 collective-permute-done.2.refs_1_
  22.5 0.7 %mats.1 = (bf16[3,1024,256]{2,1,0:T(8,128)(2,1)S(1)}, bf16[512,256]{1,0:T(8,128)(2,1)S(1)}, bf16[128,1024]{1,0:T(8,128)(2,1)S(1)}) custom-call(bf16[4,6,256,128]{3,2,1,0:T(8,128)(2,1)S(1)} %get-tuple-element.20.after_ref.near_ref, bf16[35,16,128]{2,1,0:T(8,128)(2,1)S(1)} %get-tuple-element.22.refs_0_, bf16[35,16,128]{2,1,0:T(8,128)(2,1)S(1)} %collective-permute-done.2.refs_1_), custom_call_target="tpu_custom_call" | custom-call | tf_op jit(solution)/shard_map/mats/pallas_call | solution.py:514
  23.1 0.0 collective-permute-done.1.halo_ref
  23.1 0.0 copy-done.4
  23.2 0.0 copy-done.5
  23.2 18.7 %head_and_grads.1 = (f32[2,19,16,128]{3,2,1,0:T(8,128)S(1)}, f32[2,19,16,128]{3,2,1,0:T(8,128)S(1)}) custom-call(s32[2,8]{1,0:T(2,128)S(1)} %copy-done.3, f32[8,512,256]{2,1,0:T(8,128)S(1)} %get-tuple-element.19.part_ref, bf16[4,24,64,128]{3,2,1,0:T(8,128)(2,1)S(1)} %collective-permute-done.1.halo_ref, ...), custom_call_target="tpu_custom_call" | custom-call | flops 38654705664 | bytes 16777216 | tf_op jit(solution)/shard_map/head_and_grads/pallas_call | solution.py:528
  41.8 0.1 collective-permute-start.3
  41.9 1.6 %collective-permute-done.3 = f32[2,19,16,128]{3,2,1,0:T(8,128)S(1)} collective-permute-done((f32[2,19,16,128]{3,2,1,0:T(8,128)S(1)}, f32[2,19,16,128]{3,2,1,0:T(8,128)S(1)}, u32[]{:S(2)}, u32[]{:S(2)}) %collective-permute-start.3) | collective-permute-done | bytes 311328 | tf_op jit(solution)/shard_map/ppermute | solution.py:554
  43.5 0.1 fusion.8
  43.6 5.9 %collective-permute-start.6 = (bf16[19,16,128]{2,1,0:T(8,128)(2,1)S(1)}, bf16[19,16,128]{2,1,0:T(8,128)(2,1)S(1)}, u32[]{:S(2)}, u32[]{:S(2)}) collective-permute-start(bf16[19,16,128]{2,1,0:T(8,128)(2,1)S(1)} %get-tuple-element.33), channel_id=1, source_target_pairs={{0,6},{2,4},{4,2},{6,0},{8,14},{10,12},{12,10},{14,8},{1,7},{3,5},... | collective-permute-start | bytes 233480 | tf_op jit(solution)/shard_map/ppermute | solution.py:567
  49.5 0.0 collective-permute-start.5
  49.5 1.3 %collective-permute-start.4 = (bf16[19,16,128]{2,1,0:T(8,128)(2,1)S(1)}, bf16[19,16,128]{2,1,0:T(8,128)(2,1)S(1)}, u32[]{:S(2)}, u32[]{:S(2)}) collective-permute-start(bf16[19,16,128]{2,1,0:T(8,128)(2,1)S(1)} %get-tuple-element.33), channel_id=1, source_target_pairs={{0,2},{2,0},{4,6},{6,4},{8,10},{10,8},{12,14},{14,12},{1,3},{3,1},... | collective-permute-start | bytes 233480 | tf_op jit(solution)/shard_map/ppermute | solution.py:567
  50.8 1.4 %collective-permute-done.6 = bf16[19,16,128]{2,1,0:T(8,128)(2,1)S(1)} collective-permute-done((bf16[19,16,128]{2,1,0:T(8,128)(2,1)S(1)}, bf16[19,16,128]{2,1,0:T(8,128)(2,1)S(1)}, u32[]{:S(2)}, u32[]{:S(2)}) %collective-permute-start.6) | collective-permute-done | bytes 77856 | tf_op jit(solution)/shard_map/ppermute | solution.py:567
  52.2 1.7 %collective-permute-done.5 = bf16[19,16,128]{2,1,0:T(8,128)(2,1)S(1)} collective-permute-done((bf16[19,16,128]{2,1,0:T(8,128)(2,1)S(1)}, bf16[19,16,128]{2,1,0:T(8,128)(2,1)S(1)}, u32[]{:S(2)}, u32[]{:S(2)}) %collective-permute-start.5) | collective-permute-done | bytes 77856 | tf_op jit(solution)/shard_map/ppermute | solution.py:567
  53.9 0.0 collective-permute-done.4
  53.9 0.1 add_add_fusion
  54.0 0.1 fusion.9
  54.1 0.1 collective-permute-start.7
  54.2 6.1 %collective-permute-done.7 = bf16[19,16,128]{2,1,0:T(8,128)(2,1)S(1)} collective-permute-done((bf16[19,16,128]{2,1,0:T(8,128)(2,1)S(1)}, bf16[19,16,128]{2,1,0:T(8,128)(2,1)S(1)}, u32[]{:S(2)}, u32[]{:S(2)}) %collective-permute-start.7) | collective-permute-done | bytes 77856 | tf_op jit(solution)/shard_map/ppermute | solution.py:573
  60.3 0.1 convert_add_fusion
  60.5 0.1 fusion.7.mine_ref
  60.6 0.1 collective-permute-start.8
  60.7 1.4 %collective-permute-done.8.peer_ref = f32[19,16,128]{2,1,0:T(8,128)S(1)} collective-permute-done((f32[19,16,128]{2,1,0:T(8,128)S(1)}, f32[19,16,128]{2,1,0:T(8,128)S(1)}, u32[]{:S(2)}, u32[]{:S(2)}) %collective-permute-start.8) | collective-permute-done | bytes 155680 | tf_op jit(solution)/shard_map/ppermute | solution.py:576
  62.0 1.5 %assemble.1 = (f32[27,32,64]{2,1,0:T(8,128)}, f32[8,32,64]{2,1,0:T(8,128)}, f32[1,64]{1,0:T(1,128)}, f32[1,1]{1,0:T(1,128)}) custom-call(s32[2,8]{1,0:T(2,128)S(1)} %copy-done.3, f32[19,16,128]{2,1,0:T(8,128)S(1)} %fusion.7.mine_ref, f32[19,16,128]{2,1,0:T(8,128)S(1)} %collective-permute-done.8.peer_ref), custom_call_target="tpu_custom_call" | custom-call | tf_op jit(solution)/shard_map/assemble/pallas_call | solution.py:578
  (4 shorter events, 0.0 us)
Async XLA Ops:
  2.3 3.3 %copy-start = (bf16[27,64,32]{1,2,0:T(8,128)(2,1)S(1)}, bf16[27,64,32]{1,2,0:T(8,128)(2,1)}, u32[]{:S(2)}) copy-start(bf16[27,64,32]{1,2,0:T(8,128)(2,1)} %param.8) | copy-start | bytes 331780
  2.4 3.3 %copy-start.1 = (bf16[27,64,32]{1,2,0:T(8,128)(2,1)S(1)}, bf16[27,64,32]{1,2,0:T(8,128)(2,1)}, u32[]{:S(2)}) copy-start(bf16[27,64,32]{1,2,0:T(8,128)(2,1)} %param.9) | copy-start | bytes 331780
  2.4 3.3 %copy-start.2 = (bf16[8,32,64]{2,1,0:T(8,128)(2,1)S(1)}, bf16[8,32,64]{2,1,0:T(8,128)(2,1)}, u32[]{:S(2)}) copy-start(bf16[8,32,64]{2,1,0:T(8,128)(2,1)} %wd_ref.1) | copy-start | bytes 98308
  2.4 5.5 %copy-start.6 = (bf16[1,64,8,24,128]{4,3,2,1,0:T(8,128)(2,1)S(1)}, bf16[1,64,8,24,128]{4,3,2,1,0:T(8,128)(2,1)}, u32[]{:S(2)}) copy-start(bf16[1,64,8,24,128]{4,3,2,1,0:T(8,128)(2,1)} %param.7) | copy-start | bytes 9437188
  3.0 20.1 %collective-permute-start.1 = (bf16[4,24,64,128]{3,2,1,0:T(8,128)(2,1)S(1)}, bf16[4,24,64,128]{3,2,1,0:T(8,128)(2,1)S(1)}, u32[]{:S(2)}, u32[]{:S(2)}) collective-permute-start(bf16[4,24,64,128]{3,2,1,0:T(8,128)(2,1)S(1)} %bitcast.34), channel_id=1, source_target_pairs={{3,2},{0,1},{6,3},{1,4},{7,6},{4,5},{10,7},{5,8},{11,10},{8,9},{14... | collective-permute-start | bytes 4718600 | tf_op jit(solution)/shard_map/ppermute | solution.py:492
  5.8 5.1 %collective-permute-start = (bf16[27,16,128]{2,1,0:T(8,128)(2,1)S(1)}, bf16[27,16,128]{2,1,0:T(8,128)(2,1)S(1)}, u32[]{:S(2)}, u32[]{:S(2)}) collective-permute-start(bf16[27,16,128]{2,1,0:T(8,128)(2,1)S(1)} %get-tuple-element.18.refs_0_), channel_id=1, source_target_pairs={{0,2},{2,0},{1,3},{3,1},{4,6},{6,4},{5,7},{7,5},{8,10},{10,8},{9,1... | collective-permute-start | bytes 331784 | tf_op jit(solution)/shard_map/ppermute | solution.py:482
  7.6 3.3 %copy-start.3 = (s32[2,8]{1,0:T(2,128)S(1)}, s32[2,8]{1,0:T(2,128)}, u32[]{:S(2)}) copy-start(s32[2,8]{1,0:T(2,128)} %foot_ref.5) | copy-start | bytes 196
  7.6 14.8 %collective-permute-start.2 = (bf16[35,16,128]{2,1,0:T(8,128)(2,1)S(1)}, bf16[35,16,128]{2,1,0:T(8,128)(2,1)S(1)}, u32[]{:S(2)}, u32[]{:S(2)}) collective-permute-start(bf16[35,16,128]{2,1,0:T(8,128)(2,1)S(1)} %get-tuple-element.22.refs_0_), channel_id=1, source_target_pairs={{0,2},{2,0},{1,3},{3,1},{4,6},{6,4},{5,7},{7,5},{8,10},{10,8},{9,1... | collective-permute-start | bytes 430088 | tf_op jit(solution)/shard_map/ppermute | solution.py:482
  22.4 0.7 %copy-start.4 = (s32[1,4,768]{2,1,0:T(4,128)S(1)}, s32[1,4,768]{2,1,0:T(4,128)}, u32[]{:S(2)}) copy-start(s32[1,4,768]{2,1,0:T(4,128)} %param.13) | copy-start | bytes 36868
  22.4 0.7 %copy-start.5 = (f32[64]{0:T(128)S(1)}, f32[64]{0:T(128)}, u32[]{:S(2)}) copy-start(f32[64]{0:T(128)} %param.11) | copy-start | bytes 772
  41.8 1.7 %collective-permute-start.3 = (f32[2,19,16,128]{3,2,1,0:T(8,128)S(1)}, f32[2,19,16,128]{3,2,1,0:T(8,128)S(1)}, u32[]{:S(2)}, u32[]{:S(2)}) collective-permute-start(f32[2,19,16,128]{3,2,1,0:T(8,128)S(1)} %get-tuple-element.27), channel_id=1, source_target_pairs={{0,1},{1,0},{2,3},{3,2},{4,5},{5,4},{6,7},{7,6},{8,9},{9,8},{10,11... | collective-permute-start | bytes 933896 | tf_op jit(solution)/shard_map/ppermute | solution.py:554
  43.6 8.6 %collective-permute-start.6 = (bf16[19,16,128]{2,1,0:T(8,128)(2,1)S(1)}, bf16[19,16,128]{2,1,0:T(8,128)(2,1)S(1)}, u32[]{:S(2)}, u32[]{:S(2)}) collective-permute-start(bf16[19,16,128]{2,1,0:T(8,128)(2,1)S(1)} %get-tuple-element.33), channel_id=1, source_target_pairs={{0,6},{2,4},{4,2},{6,0},{8,14},{10,12},{12,10},{14,8},{1,7},{3,5},... | collective-permute-start | bytes 233480 | tf_op jit(solution)/shard_map/ppermute | solution.py:567
  49.5 4.4 %collective-permute-start.5 = (bf16[19,16,128]{2,1,0:T(8,128)(2,1)S(1)}, bf16[19,16,128]{2,1,0:T(8,128)(2,1)S(1)}, u32[]{:S(2)}, u32[]{:S(2)}) collective-permute-start(bf16[19,16,128]{2,1,0:T(8,128)(2,1)S(1)} %get-tuple-element.32), channel_id=1, source_target_pairs={{0,4},{2,6},{4,0},{6,2},{8,12},{10,14},{12,8},{14,10},{1,5},{3,7},... | collective-permute-start | bytes 233480 | tf_op jit(solution)/shard_map/ppermute | solution.py:567
  49.5 4.4 %collective-permute-start.4 = (bf16[19,16,128]{2,1,0:T(8,128)(2,1)S(1)}, bf16[19,16,128]{2,1,0:T(8,128)(2,1)S(1)}, u32[]{:S(2)}, u32[]{:S(2)}) collective-permute-start(bf16[19,16,128]{2,1,0:T(8,128)(2,1)S(1)} %get-tuple-element.33), channel_id=1, source_target_pairs={{0,2},{2,0},{4,6},{6,4},{8,10},{10,8},{12,14},{14,12},{1,3},{3,1},... | collective-permute-start | bytes 233480 | tf_op jit(solution)/shard_map/ppermute | solution.py:567
  54.1 6.2 %collective-permute-start.7 = (bf16[19,16,128]{2,1,0:T(8,128)(2,1)S(1)}, bf16[19,16,128]{2,1,0:T(8,128)(2,1)S(1)}, u32[]{:S(2)}, u32[]{:S(2)}) collective-permute-start(bf16[19,16,128]{2,1,0:T(8,128)(2,1)S(1)} %fusion.9), channel_id=1, source_target_pairs={{0,8},{4,12},{8,0},{12,4},{1,9},{5,13},{9,1},{13,5},{2,10},{6,14},... | collective-permute-start | bytes 233480 | tf_op jit(solution)/shard_map/ppermute | solution.py:573
  60.6 1.4 %collective-permute-start.8 = (f32[19,16,128]{2,1,0:T(8,128)S(1)}, f32[19,16,128]{2,1,0:T(8,128)S(1)}, u32[]{:S(2)}, u32[]{:S(2)}) collective-permute-start(f32[19,16,128]{2,1,0:T(8,128)S(1)} %fusion.7.mine_ref), channel_id=1, source_target_pairs={{0,1},{1,0},{2,3},{3,2},{4,5},{5,4},{6,7},{7,6},{8,9},{9,8},{10,11... | collective-permute-start | bytes 466952 | tf_op jit(solution)/shard_map/ppermute | solution.py:576
